TPU v7x, 768 devices: a whole 4x8x12 slice. The times are simulated.
768 devices in a mesh: grp: 24 (over z, core), dev: 32 (over x, y).
Axes of the slice: x: 4, y: 8, z: 12, core: 2. Of those that a mesh axis runs over, the one named last changes fastest.
Arguments:
- tracer: float32 [72, 16, 98304], P(None, None, ('grp', 'dev')), may hold values from -6 to 6
- metric: float32 [98304], P(('grp', 'dev')), may hold values from 0.5 to 2
- coef: float32 [72, 1572864], P(None, ('grp', 'dev')), may hold values from 0.02 to 601
- nbr_slot: int32 [4, 98304], P(None, ('grp', 'dev')), may hold values from 0 to 559, as said below
- edge_flip: int32 [4, 98304], P(None, ('grp', 'dev')), may hold values from 0 to 1, as said below
- send_slot: int32 [36864], P(('grp', 'dev')), may hold values from 0 to 511, as said below
- span_slot: int32 [16, 98304], P(None, ('grp', 'dev')), may hold values from 0 to 65535, as said below
Outputs:
- mixed: float32 [72, 16, 98304], P(None, None, ('grp', 'dev'))
Inputs may be any that keep to these rules, and one draw needn't show every extreme that they name: `nbr_slot`: entries below 512 name an edge of an element of the same device as s * 128 + e; larger ones name the neighbouring devices' buffer entries in the order of the edge table. Each element edge meets exactly one other edge, both ways. `edge_flip`: symmetric over the two sides of a shared edge. `send_slot`: each entry is an own edge s * 128 + e'. For each device, 16 own edges whose neighbours lie on device (g + 1, v), 16 for (g - 1, v), 8 for (g, v + 1), 8 for (g, v - 1), in the order the receiving edge table expects. `span_slot`: within each group along dev the values form a permutation of 0 to 65535, and every device holds exactly 64 columns whose value lies in each range r * 2048 to (r + 1) * 2048 - 1.
All inputs are finite; a program needn't handle non-finite values.
Results may differ from a plain program's by a relative error of at most 0.0003.
Values sent between devices are 32-bit elements; how exact they have to be, the bound alone decides.
No kernel may reach another device: no remote copies, remote signals or barrier semaphores. Data moves between devices by JAX's collectives and lax.ppermute only.
A program may use at most 32 MiB of HBM per device.

v0:
```python
import jax
import jax.numpy as jnp
import numpy as np
from jax import lax
from jax.sharding import PartitionSpec as P

BR = 8
BC = 16


PENALTY = 10.0
HYPER = 0.0001


def padded(value, sides, width):
    for axis, dim in sides:
        size, length = (lax.axis_size(axis), value.shape[dim])
        up = [(i, (i + 1) % size) for i in range(size)]
        down = [(j, i) for i, j in up]
        last = lax.slice_in_dim(value, length - width, length, axis=dim)
        first = lax.slice_in_dim(value, 0, width, axis=dim)
        before = lax.ppermute(last, axis, up)
        after = lax.ppermute(first, axis, down)
        value = jnp.concatenate([before, value, after], axis=dim)
    return value


def gll_tables():
    gll_nodes = np.array([-1.0, -1.0 / np.sqrt(5.0), 1.0 / np.sqrt(5.0), 1.0])
    weights = np.array([1.0 / 6.0, 5.0 / 6.0, 5.0 / 6.0, 1.0 / 6.0])
    lambdas = np.ones(4)
    for jdx in range(4):
        for kdx in range(4):
            if kdx != jdx:
                lambdas[jdx] = lambdas[jdx] / (gll_nodes[jdx] - gll_nodes[kdx])
    derivative = np.zeros((4, 4))
    for idx in range(4):
        for jdx in range(4):
            if idx != jdx:
                derivative[idx, jdx] = (
                    lambdas[jdx] / lambdas[idx] / (gll_nodes[idx] - gll_nodes[jdx])
                )
        derivative[idx, idx] = -np.sum(derivative[idx])
    stiffness = -(derivative.T * weights[None, :] @ derivative) / weights[:, None]
    identity = np.eye(4)
    lap_matrix = np.kron(stiffness, identity) + np.kron(identity, stiffness)
    edge_points = np.array([[0, 1, 2, 3], [3, 7, 11, 15], [12, 13, 14, 15], [0, 4, 8, 12]])
    edge_order = edge_points.T.reshape(-1)
    spread = np.zeros((16, 16))
    spread[edge_order, np.arange(16)] = 1.0
    return (lap_matrix.astype(np.float32), spread.astype(np.float32), edge_order.astype(np.int32))


def element_operator(block_field, elem_scale, neighbours, flip_bits, send_list):
    lap_matrix, spread, edge_order = gll_tables()
    levels, points, elem_count = block_field.shape
    own_edges = jnp.take(block_field, jnp.asarray(edge_order), axis=1).reshape(
        levels, 4, 4 * elem_count
    )
    outgoing = jnp.take(own_edges, send_list, axis=2)
    row_out = jnp.stack([outgoing[:, :, BC : 2 * BC], outgoing[:, :, :BC]])
    row_in = padded(row_out, (("grp", 0),), 1)
    col_out = jnp.stack([outgoing[:, :, 2 * BC + BR :], outgoing[:, :, 2 * BC : 2 * BC + BR]])
    col_in = padded(col_out, (("dev", 0),), 1)
    inner_part = jnp.einsum(
        "pq,lqe->lpe", jnp.asarray(lap_matrix), block_field, precision=lax.Precision.HIGHEST
    )
    edge_table = jnp.concatenate([own_edges, row_in[0], row_in[3], col_in[0], col_in[3]], axis=2)
    across = jnp.take(edge_table, neighbours, axis=2)
    across = jnp.where(flip_bits[None, None, :] == 1, across[:, ::-1, :], across)
    jump_terms = (PENALTY * (across - own_edges)).reshape(levels, 16, elem_count)
    edge_part = jnp.einsum(
        "pk,lke->lpe", jnp.asarray(spread), jump_terms, precision=lax.Precision.HIGHEST
    )
    return elem_scale[None, None, :] * (inner_part + edge_part)


def vertical_solve(values, mixing):
    columns = values.shape[1]
    mixing_below = jnp.concatenate([mixing[1:], jnp.zeros((1, columns), jnp.float32)], axis=0)
    diagonal = 1.0 + mixing + mixing_below
    sub_diag = jnp.concatenate([jnp.zeros((1, columns), jnp.float32), -mixing[1:]], axis=0)
    super_diag = -mixing_below

    def forward(carry, level_in):
        upper_prev, rhs_prev = carry
        sub_here, diag_here, sup_here, rhs_here = level_in
        denom = diag_here - sub_here * upper_prev
        upper_now = sup_here / denom
        rhs_now = (rhs_here - sub_here * rhs_prev) / denom
        return ((upper_now, rhs_now), (upper_now, rhs_now))

    start = (jnp.zeros((columns,), jnp.float32), jnp.zeros((columns,), jnp.float32))
    ignored, (uppers, rhs_mod) = lax.scan(forward, start, (sub_diag, diagonal, super_diag, values))

    def backward(below, level_in):
        upper_here, rhs_here = level_in
        solved_here = rhs_here - upper_here * below
        return (solved_here, solved_here)

    ignored_too, solved = lax.scan(
        backward, jnp.zeros((columns,), jnp.float32), (uppers, rhs_mod), reverse=True
    )
    return solved


def on_device(tracer, metric, coef, nbr_slot, edge_flip, send_slot, span_slot):
    neighbours = nbr_slot.reshape(-1)
    flip_bits = edge_flip.reshape(-1)
    first_pass = element_operator(tracer, metric, neighbours, flip_bits, send_slot)
    second = element_operator(first_pass, metric, neighbours, flip_bits, send_slot)
    stepped = tracer - HYPER * second
    levels = tracer.shape[0]
    col_count = tracer.shape[1] * tracer.shape[2]
    group_size = lax.axis_size("dev")
    per_peer = col_count // group_size
    span_ids = span_slot.reshape(-1)
    target_dev = span_ids // col_count
    target_pos = span_ids % col_count
    dest_hits = (jnp.arange(group_size, dtype=jnp.int32)[:, None] == target_dev[None, :]).astype(
        jnp.int32
    )
    arrival = jnp.sum((jnp.cumsum(dest_hits, axis=1) - dest_hits) * dest_hits, axis=0)
    bucket = target_dev * per_peer + arrival
    send_order = (
        jnp.zeros((col_count,), jnp.int32).at[bucket].set(jnp.arange(col_count, dtype=jnp.int32))
    )
    sent_pos = jnp.take(target_pos, send_order)[None, :]
    columns = stepped.reshape(levels, col_count)
    sent_cols = jnp.take(columns, send_order, axis=1)
    got_cols, got_pos = (
        lax.all_to_all(sent_cols, "dev", split_axis=1, concat_axis=1, tiled=True),
        lax.all_to_all(
            sent_pos.astype(jnp.float32), "dev", split_axis=1, concat_axis=1, tiled=True
        ),
    )
    mixing = jnp.take(coef, got_pos[0].astype(jnp.int32), axis=1)
    solved = vertical_solve(got_cols, mixing)
    returned = lax.all_to_all(solved, "dev", split_axis=1, concat_axis=1, tiled=True)
    mixed_out = jnp.take(returned, bucket, axis=1)
    return mixed_out.reshape(tracer.shape)


def solution(mesh):
    in_specs = (
        P(None, None, ("grp", "dev")),
        P(("grp", "dev")),
        P(None, ("grp", "dev")),
        P(None, ("grp", "dev")),
        P(None, ("grp", "dev")),
        P(("grp", "dev")),
        P(None, ("grp", "dev")),
    )
    out_specs = P(None, None, ("grp", "dev"))
    return jax.shard_map(
        on_device, mesh=mesh, in_specs=in_specs, out_specs=out_specs, check_vma=False
    )
```

profile of v0, /device:TPU:8, one launch (start us, length us, event | category | flops | bytes accessed | tf_op | source)
XLA Modules:
  0.0 320.2 jit_solution(11990215852852626962)
XLA Ops:
  2.0 2.1 gather_fusion.2
  5.7 12.1 %collective-permute-start.1 = (f32[1,72,4,16]{1,2,3,0:T(4,128)S(1)}, f32[1,72,4,16]{1,2,3,0:T(4,128)S(1)}, u32[]{:S(2)}, u32[]{:S(2)}) collective-permute-start(f32[1,72,4,16]{1,2,3,0:T(4,128)S(1)} %get-tuple-element.315), channel_id=1, source_target_pairs={{32,0},{64,32},{96,64},{128,96},{160,128},{192,160},{224,192},{256... | collective-permute-start | bytes 55304 | tf_op jit(solution)/shard_map/ppermute | solution.py:23
  18.4 3.5 %collective-permute-start.2 = (f32[1,72,4,8]{1,2,3,0:T(4,128)}, f32[1,72,4,8]{1,2,3,0:T(4,128)S(1)}, u32[]{:S(2)}, u32[]{:S(2)}) collective-permute-start(f32[1,72,4,8]{1,2,3,0:T(4,128)} %get-tuple-element.314), channel_id=1, source_target_pairs={{0,1},{1,2},{2,3},{3,4},{4,5},{5,6},{6,7},{7,8},{8,9},{9,10},{10,1... | collective-permute-start | bytes 27656 | tf_op jit(solution)/shard_map/ppermute | solution.py:22
  21.9 2.4 collective-permute-start.3
  24.3 9.1 %reduce-window.6 = s32[32,16,128]{2,1,0:T(8,128)S(1)} reduce-window(s32[32,16,128]{2,1,0:T(8,128)S(1)} %fusion.15, s32[]{:T(128)} %constant.144.clone.1), window={size=1x1x128 pad=0_0x0_0x127_0}, to_apply=%region_0.1 | reduce-window | flops 8323072 | bytes 524292 | tf_op jit(solution)/shard_map/reduce-window
  34.2 8.0 %scatter_custom_fusion = s32[2048]{0:T(1024)S(1)} fusion(s32[2048]{0:T(1024)S(1)} %bitcast.162, s32[2048]{0:T(1024)S(1)} %iota.14, s32[]{:T(128)} %constant.144.clone.1), kind=kCustom, calls=%fused_computation.109 | custom fusion | bytes 8196 | tf_op jit(solution)/shard_map/scatter | solution.py:126
  42.3 11.8 %gather_fusion = s32[2048]{0:T(1024)S(1)} fusion(s32[2048]{0:T(1024)S(1)} %get-tuple-element.319, s32[2048]{0:T(1024)S(1)} %get-tuple-element.320), kind=kCustom, calls=%fused_computation.9 | custom fusion | bytes 24576 | tf_op jit(solution)/shard_map/jit(_take)/gather | solution.py:128
  55.4 11.4 %all-to-all-start = ((f32[1,32,64]{2,0,1:T(1,128)}), f32[1,32,64]{2,0,1:T(1,128)S(1)}, u32[]{:S(2)}, u32[]{:S(2)}) async-start(f32[1,32,64]{2,0,1:T(1,128)} %convert_element_type.28), calls=%async_computation | async-start | bytes 32768 | tf_op jit(solution)/shard_map/all_to_all | solution.py:133
  69.0 1.4 convolution_bitcast_fusion
  70.8 4.6 %all-to-all-done = f32[1,32,64]{2,0,1:T(1,128)S(1)} async-done(((f32[1,32,64]{2,0,1:T(1,128)}), f32[1,32,64]{2,0,1:T(1,128)S(1)}, u32[]{:S(2)}, u32[]{:S(2)}) %all-to-all-start) | async-done | bytes 8224 | tf_op jit(solution)/shard_map/all_to_all | solution.py:133
  75.5 5.5 %gather_fusion.1 = f32[2048,72]{1,0:T(8,128)S(1)} fusion(f32[72,2048]{0,1:T(8,128)S(1)} %copy.100, s32[2048]{0:T(1024)S(1)} %fusion.23), kind=kCustom, calls=%fused_computation.clone | custom fusion | bytes 1187840 | tf_op jit(solution)/shard_map/jit(_take)/gather | solution.py:137
  83.4 2.8 gather_fusion.4
  90.3 1.7 fusion.10
  94.5 2.0 gather_fusion.6
  96.7 1.4 fusion.27
  99.2 3.0 collective-permute-start.5
  102.1 2.5 collective-permute-start.6
  104.6 3.5 %collective-permute-start.7 = (f32[1,72,4,8]{1,2,3,0:T(4,128)S(1)}, f32[1,72,4,8]{1,2,3,0:T(4,128)S(1)}, u32[]{:S(2)}, u32[]{:S(2)}) collective-permute-start(f32[1,72,4,8]{1,2,3,0:T(4,128)S(1)} %get-tuple-element.309), channel_id=1, source_target_pairs={{1,0},{2,1},{3,2},{4,3},{5,4},{6,5},{7,6},{8,7},{9,8},{10,9},{11,1... | collective-permute-start | bytes 27656 | tf_op jit(solution)/shard_map/ppermute | solution.py:23
  110.9 2.8 gather_fusion.7
  117.6 1.7 fusion.8
  119.7 5.5 %gather_fusion.8 = f32[2048,72]{1,0:T(8,128)S(1)} fusion(f32[72,2048]{0,1:T(8,128)S(1)} %bitcast.144, s32[2048]{0:T(1024)S(1)} %get-tuple-element.320), kind=kCustom, calls=%fused_computation.4.clone | custom fusion | bytes 1187840 | tf_op jit(solution)/shard_map/jit(_take)/gather | solution.py:130
  125.2 1.3 broadcast_select_fusion.1
  126.5 10.9 %all-to-all-start.1 = ((f32[72,32,64]{0,2,1:T(8,128)}), f32[72,32,64]{0,2,1:T(8,128)S(1)}, u32[]{:S(2)}, u32[]{:S(2)}) async-start(f32[72,32,64]{0,2,1:T(8,128)} %bitcast.39), calls=%async_computation.1 | async-start | bytes 2097152 | tf_op jit(solution)/shard_map/all_to_all | solution.py:132
  138.1 1.5 add_add_fusion
  139.6 2.4 copy.115
  143.6 18.7 %all-to-all-done.1 = f32[72,32,64]{0,2,1:T(8,128)S(1)} async-done(((f32[72,32,64]{0,2,1:T(8,128)}), f32[72,32,64]{0,2,1:T(8,128)S(1)}, u32[]{:S(2)}, u32[]{:S(2)}) %all-to-all-start.1) | async-done | bytes 589856 | tf_op jit(solution)/shard_map/all_to_all | solution.py:132
  162.7 99.8 %while.34 = (s32[]{:T(128)}, f32[2048]{0:T(1024)S(1)}, f32[2048]{0:T(1024)S(1)}, f32[72,2048]{1,0:T(8,128)S(1)}, f32[72,2048]{1,0:T(8,128)S(1)}, /*index=5*/f32[...) while((s32[]{:T(128)}, f32[2048]{0:T(1024)S(1)}, ...), condition=%wide.region_5.10_spmd.clone, body=%wide.region_4.9_spmd.clone.sunk | while | flops 16387 | bytes 163975 | solution.py:94
  262.6 19.9 %while.35 = (s32[]{:T(128)}, f32[2048]{0:T(1024)S(1)}, f32[72,2048]{1,0:T(8,128)S(1)}, f32[72,2048]{1,0:T(8,128)S(1)}, f32[72,2048]{1,0:T(8,128)S(1)}, /*index=5*/s32[]{:T(128)}, s32[]{:T(128)}, s32[]{:T(128)}) while((s32[]{:T(128)}, f32[2048]{0:T(1024)S(1)}, f32[72,2048]{1,0:T(8,128)S(1)}, f32[72,2048]{1,0:T(8,128)S(1)}, ...), condition=%wide.region_7.12_spmd.clone, body=%wide.region_6.11_spmd.clone.sunk | while | flops 6148 | bytes 82035 | solution.py:101
  282.4 1.3 copy.123
  283.8 5.2 %all-to-all-start.2 = ((f32[72,32,64]{0,2,1:T(8,128)}), f32[72,32,64]{0,2,1:T(8,128)S(1)}, u32[]{:S(2)}, u32[]{:S(2)}) async-start(f32[72,32,64]{0,2,1:T(8,128)} %bitcast.41), calls=%async_computation.2 | async-start | bytes 2097152 | tf_op jit(solution)/shard_map/all_to_all | solution.py:139
  289.0 24.2 %all-to-all-done.2 = f32[72,32,64]{0,2,1:T(8,128)S(1)} async-done(((f32[72,32,64]{0,2,1:T(8,128)}), f32[72,32,64]{0,2,1:T(8,128)S(1)}, u32[]{:S(2)}, u32[]{:S(2)}) %all-to-all-start.2) | async-done | bytes 589856 | tf_op jit(solution)/shard_map/all_to_all | solution.py:139
  313.2 5.5 %gather_fusion.9 = f32[2048,72]{1,0:T(8,128)S(1)} fusion(f32[72,2048]{0,1:T(8,128)S(1)} %bitcast.143, s32[2048]{0:T(1024)S(1)} %broadcast_clamp_fusion), kind=kCustom, calls=%fused_computation.5.clone | custom fusion | bytes 1187840 | tf_op jit(solution)/shard_map/jit(_take)/gather | solution.py:140
  (698 shorter events, 143.0 us)
Async XLA Ops:
  1.3 4.2 %copy-start.15 = (pred[48]{0:T(512)(128)(4,1)}, pred[48]{0:T(512)(128)(4,1)S(1)}, u32[]{:S(2)}) copy-start(pred[48]{0:T(512)(128)(4,1)S(1)} %compare_and_fusion.4) | copy-start | bytes 148
  2.0 2.1 copy-start.12
  2.0 2.9 copy-start.11
  4.3 20.0 %copy-start.6 = (s32[16,128]{1,0:T(8,128)S(1)}, s32[16,128]{1,0:T(8,128)}, u32[]{:S(2)}) copy-start(s32[16,128]{1,0:T(8,128)} %param.31) | copy-start | bytes 24580
  5.7 75.3 %collective-permute-start = (f32[1,72,4,16]{1,2,3,0:T(4,128)S(1)}, f32[1,72,4,16]{1,2,3,0:T(4,128)S(1)}, u32[]{:S(2)}, u32[]{:S(2)}) collective-permute-start(f32[1,72,4,16]{1,2,3,0:T(4,128)S(1)} %get-tuple-element.316), channel_id=1, source_target_pairs={{0,32},{32,64},{64,96},{96,128},{128,160},{160,192},{192,224},{224... | collective-permute-start | bytes 55304 | tf_op jit(solution)/shard_map/ppermute | solution.py:22
  5.7 75.9 %collective-permute-start.1 = (f32[1,72,4,16]{1,2,3,0:T(4,128)S(1)}, f32[1,72,4,16]{1,2,3,0:T(4,128)S(1)}, u32[]{:S(2)}, u32[]{:S(2)}) collective-permute-start(f32[1,72,4,16]{1,2,3,0:T(4,128)S(1)} %get-tuple-element.315), channel_id=1, source_target_pairs={{32,0},{64,32},{96,64},{128,96},{160,128},{192,160},{224,192},{256... | collective-permute-start | bytes 55304 | tf_op jit(solution)/shard_map/ppermute | solution.py:23
  18.4 63.8 %collective-permute-start.2 = (f32[1,72,4,8]{1,2,3,0:T(4,128)}, f32[1,72,4,8]{1,2,3,0:T(4,128)S(1)}, u32[]{:S(2)}, u32[]{:S(2)}) collective-permute-start(f32[1,72,4,8]{1,2,3,0:T(4,128)} %get-tuple-element.314), channel_id=1, source_target_pairs={{0,1},{1,2},{2,3},{3,4},{4,5},{5,6},{6,7},{7,8},{8,9},{9,10},{10,1... | collective-permute-start | bytes 27656 | tf_op jit(solution)/shard_map/ppermute | solution.py:22
  21.9 60.9 %collective-permute-start.3 = (f32[1,72,4,8]{1,2,3,0:T(4,128)S(1)}, f32[1,72,4,8]{1,2,3,0:T(4,128)S(1)}, u32[]{:S(2)}, u32[]{:S(2)}) collective-permute-start(f32[1,72,4,8]{1,2,3,0:T(4,128)S(1)} %get-tuple-element.313), channel_id=1, source_target_pairs={{1,0},{2,1},{3,2},{4,3},{5,4},{6,5},{7,6},{8,7},{9,8},{10,9},{11,1... | collective-permute-start | bytes 27656 | tf_op jit(solution)/shard_map/ppermute | solution.py:23
  54.1 13.8 %copy-start.10 = (s32[4,128]{1,0:T(4,128)S(1)}, s32[4,128]{1,0:T(4,128)}, u32[]{:S(2)}) copy-start(s32[4,128]{1,0:T(4,128)} %param.28) | copy-start | bytes 6148
  54.1 14.4 %copy-start.17 = (s32[4,128]{1,0:T(4,128)S(1)}, s32[4,128]{1,0:T(4,128)}, u32[]{:S(2)}) copy-start(s32[4,128]{1,0:T(4,128)} %param.29) | copy-start | bytes 6148
  54.1 14.9 %copy-start = (f32[72,16,128]{2,1,0:T(8,128)S(1)}, f32[72,16,128]{2,1,0:T(8,128)}, u32[]{:S(2)}) copy-start(f32[72,16,128]{2,1,0:T(8,128)} %param.25) | copy-start | bytes 1769476
  54.1 14.9 %copy-start.7 = (f32[16,16,1]{1,0,2:T(8,128)S(1)}, f32[16,16,1]{1,0,2:T(8,128)}, u32[]{:S(2)}) copy-start(f32[16,16,1]{1,0,2:T(8,128)} %constant.190) | copy-start | bytes 3076
  55.4 20.0 %all-to-all-start = ((f32[1,32,64]{2,0,1:T(1,128)}), f32[1,32,64]{2,0,1:T(1,128)S(1)}, u32[]{:S(2)}, u32[]{:S(2)}) async-start(f32[1,32,64]{2,0,1:T(1,128)} %convert_element_type.28), calls=%async_computation | async-start | bytes 32768 | tf_op jit(solution)/shard_map/all_to_all | solution.py:133
  67.8 2.6 copy-start.5
  83.4 4.0 %copy-start.13 = (pred[512]{0:T(512)(128)(4,1)S(1)}, pred[512]{0:T(512)(128)(4,1)}, u32[]{:S(2)}) copy-start(pred[512]{0:T(512)(128)(4,1)} %compare_and_fusion.3) | copy-start | bytes 1540
  86.2 2.3 copy-start.14
  88.8 1.5 copy-start.4
  88.8 1.5 copy-start.8
  88.8 1.5 copy-start.18
  93.2 3.3 %copy-start.16 = (pred[48]{0:T(512)(128)(4,1)S(1)}, pred[48]{0:T(512)(128)(4,1)}, u32[]{:S(2)}) copy-start(pred[48]{0:T(512)(128)(4,1)} %copy-done.15) | copy-start | bytes 148
  96.5 1.6 copy-start.1
  98.1 10.0 %collective-permute-start.4 = (f32[1,72,4,16]{1,2,3,0:T(4,128)S(1)}, f32[1,72,4,16]{1,2,3,0:T(4,128)S(1)}, u32[]{:S(2)}, u32[]{:S(2)}) collective-permute-start(f32[1,72,4,16]{1,2,3,0:T(4,128)S(1)} %get-tuple-element.312), channel_id=1, source_target_pairs={{0,32},{32,64},{64,96},{96,128},{128,160},{160,192},{192,224},{224... | collective-permute-start | bytes 55304 | tf_op jit(solution)/shard_map/ppermute | solution.py:22
  99.2 9.6 %collective-permute-start.5 = (f32[1,72,4,16]{1,2,3,0:T(4,128)S(1)}, f32[1,72,4,16]{1,2,3,0:T(4,128)S(1)}, u32[]{:S(2)}, u32[]{:S(2)}) collective-permute-start(f32[1,72,4,16]{1,2,3,0:T(4,128)S(1)} %get-tuple-element.311), channel_id=1, source_target_pairs={{32,0},{64,32},{96,64},{128,96},{160,128},{192,160},{224,192},{256... | collective-permute-start | bytes 55304 | tf_op jit(solution)/shard_map/ppermute | solution.py:23
  102.1 7.3 %collective-permute-start.6 = (f32[1,72,4,8]{1,2,3,0:T(4,128)S(1)}, f32[1,72,4,8]{1,2,3,0:T(4,128)S(1)}, u32[]{:S(2)}, u32[]{:S(2)}) collective-permute-start(f32[1,72,4,8]{1,2,3,0:T(4,128)S(1)} %get-tuple-element.310), channel_id=1, source_target_pairs={{0,1},{1,2},{2,3},{3,4},{4,5},{5,6},{6,7},{7,8},{8,9},{9,10},{10,1... | collective-permute-start | bytes 27656 | tf_op jit(solution)/shard_map/ppermute | solution.py:22
  104.6 5.6 %collective-permute-start.7 = (f32[1,72,4,8]{1,2,3,0:T(4,128)S(1)}, f32[1,72,4,8]{1,2,3,0:T(4,128)S(1)}, u32[]{:S(2)}, u32[]{:S(2)}) collective-permute-start(f32[1,72,4,8]{1,2,3,0:T(4,128)S(1)} %get-tuple-element.309), channel_id=1, source_target_pairs={{1,0},{2,1},{3,2},{4,3},{5,4},{6,5},{7,6},{8,7},{9,8},{10,9},{11,1... | collective-permute-start | bytes 27656 | tf_op jit(solution)/shard_map/ppermute | solution.py:23
  116.2 1.5 copy-start.3
  119.7 5.5 %copy-start.9 = (pred[2048]{0:T(1024)(128)(4,1)S(1)}, pred[2048]{0:T(1024)(128)(4,1)}, u32[]{:S(2)}) copy-start(pred[2048]{0:T(1024)(128)(4,1)} %get-tuple-element.296) | copy-start | bytes 6148
  126.5 35.7 %all-to-all-start.1 = ((f32[72,32,64]{0,2,1:T(8,128)}), f32[72,32,64]{0,2,1:T(8,128)S(1)}, u32[]{:S(2)}, u32[]{:S(2)}) async-start(f32[72,32,64]{0,2,1:T(8,128)} %bitcast.39), calls=%async_computation.1 | async-start | bytes 2097152 | tf_op jit(solution)/shard_map/all_to_all | solution.py:132
  139.6 2.5 copy-start.2
  283.8 29.4 %all-to-all-start.2 = ((f32[72,32,64]{0,2,1:T(8,128)}), f32[72,32,64]{0,2,1:T(8,128)S(1)}, u32[]{:S(2)}, u32[]{:S(2)}) async-start(f32[72,32,64]{0,2,1:T(8,128)} %bitcast.41), calls=%async_computation.2 | async-start | bytes 2097152 | tf_op jit(solution)/shard_map/all_to_all | solution.py:139
where the time goes:
time: 325 us; the launch traced here: 320 us
  local copies, waits for them, and re-layouts  183 us (56%)
  starting transfers between devices  54.4 us (17%)
  waiting for transfers between devices  47.8 us (15%)
  other arithmetic  21.5 us (7%)
  loops' own time  6.86 us (2%)
  matrix products  6.3 us (2%)
    dynamic_slice x216, local copies, waits for them, and re-layouts, vertical_solve(): lax.scan(forward, start, (sub_diag, diagonal, super_diag, values))  67.1 us
    dynamic_update_slice x216, local copies, waits for them, and re-layouts, vertical_solve(): lax.scan(forward, start, (sub_diag, diagonal, super_diag, values))  44.3 us
    all_to_all x1, waiting for transfers between devices, on_device(): lax.all_to_all(solved, 'dev', split_axis=1, concat_axis=1, tiled=True)  24.2 us
    ppermute x4, starting transfers between devices, padded(): after = lax.ppermute(first, axis, down)  20.9 us
    all_to_all x1, waiting for transfers between devices, on_device(): lax.all_to_all(sent_cols, 'dev', split_axis=1, concat_axis=1, tiled=True)  18.7 us
    gather x1, local copies, waits for them, and re-layouts, on_device(): sent_pos = jnp.take(target_pos, send_order)[None, :]  11.8 us
    all_to_all x1, starting transfers between devices, on_device(): lax.all_to_all(sent_pos.astype(jnp.float32), 'dev', split_axis=1, concat_...  11.4 us
    all_to_all x1, starting transfers between devices, on_device(): lax.all_to_all(sent_cols, 'dev', split_axis=1, concat_axis=1, tiled=True)  10.9 us
  transfers between devices with their start and end apart: 11, of which 4 were waited for; matrix products, arithmetic and copies ran while one was open for 16% of the time, Pallas kernels for 0%

commit v1 on v0

v1 whole, which is shorter than its diff:
```python
import jax
import jax.numpy as jnp
import numpy as np
from jax import lax
from jax.experimental import pallas as pl
from jax.experimental.pallas import tpu as pltpu
from jax.sharding import PartitionSpec as P

BR = 8
BC = 16
LEV = 72
PTS = 16
ELEM = 128
COLS = PTS * ELEM
PEERS = 32
PER = COLS // PEERS
ROWS = 40
BLOCKS = LEV // 8

PENALTY = 10.0
HYPER = 0.0001

VMEM = pl.BlockSpec(memory_space=pltpu.VMEM)
SMEM = pl.BlockSpec(memory_space=pltpu.SMEM)
PARAMS = pltpu.CompilerParams(vmem_limit_bytes=8 << 20)

EDGE_POINT = [[0, 1, 2, 3], [3, 7, 11, 15], [12, 13, 14, 15], [0, 4, 8, 12]]


def stiffness():
    nodes = np.array([-1.0, -1.0 / np.sqrt(5.0), 1.0 / np.sqrt(5.0), 1.0])
    weights = np.array([1.0 / 6.0, 5.0 / 6.0, 5.0 / 6.0, 1.0 / 6.0])
    lambdas = np.ones(4)
    for j in range(4):
        for k in range(4):
            if k != j:
                lambdas[j] = lambdas[j] / (nodes[j] - nodes[k])
    deriv = np.zeros((4, 4))
    for i in range(4):
        for j in range(4):
            if i != j:
                deriv[i, j] = lambdas[j] / lambdas[i] / (nodes[i] - nodes[j])
        deriv[i, i] = -np.sum(deriv[i])
    return -(deriv.T * weights[None, :] @ deriv) / weights[:, None]


def iota(shape, dim):
    return lax.broadcasted_iota(jnp.int32, shape, dim)


def parts_of(value):
    high = value.astype(jnp.bfloat16)
    low = (value - high.astype(jnp.float32)).astype(jnp.bfloat16)
    return jnp.concatenate([high, low], axis=0)


def moved(stacked, hot):
    product = jnp.dot(stacked, hot, preferred_element_type=jnp.float32)
    half = product.shape[0] // 2
    return product[:half] + product[half:]


def one_hot(index, depth):
    width = index.shape[1]
    low, high = index & (ELEM - 1), index >> 7
    base = jnp.broadcast_to(low, (ELEM, width)) == iota((ELEM, width), 0)
    base = jnp.where(base, 1.0, 0.0).astype(jnp.bfloat16)
    return jnp.concatenate(
        [
            base * jnp.broadcast_to(jnp.where(high == h, 1.0, 0.0), (ELEM, width)).astype(jnp.bfloat16)
            for h in range(depth // ELEM)
        ],
        axis=0,
    )


def inside(value):
    return pltpu.with_memory_space_constraint(value, pltpu.VMEM)


def route_kernel(span_ref, req_ref, bucket_ref):
    span = span_ref[...]
    target = span >> 11
    pos = span & (COLS - 1)
    peer = iota((PEERS, ELEM), 0)
    hot = [
        jnp.where(jnp.broadcast_to(target[p : p + 1], (PEERS, ELEM)) == peer, 1.0, 0.0)
        for p in range(PTS)
    ]
    stacked = jnp.concatenate(hot, axis=0).astype(jnp.bfloat16)
    row, col = iota((ELEM, 2 * ELEM), 0), iota((ELEM, 2 * ELEM), 1)
    ahead = jnp.where((row < col) | (col >= ELEM), 1.0, 0.0).astype(jnp.bfloat16)
    counts = jnp.dot(stacked, ahead, preferred_element_type=jnp.float32)
    base = jnp.zeros((PEERS, ELEM), jnp.float32)
    arrivals = []
    for p in range(PTS):
        here = counts[p * PEERS : (p + 1) * PEERS]
        arrivals.append(jnp.sum(hot[p] * (here[:, :ELEM] + base), axis=0, keepdims=True))
        base = base + here[:, ELEM:]
    arrival = jnp.concatenate(arrivals, axis=0).astype(jnp.int32)
    bucket_ref[...] = target * PER + arrival
    high = (pos >> 8).astype(jnp.float32)
    low = (pos & 255).astype(jnp.float32)
    slot = iota((PER, ELEM), 0)
    left, right = [], []
    for p in range(PTS):
        left.append(
            jnp.concatenate([hot[p] * high[p : p + 1], hot[p] * low[p : p + 1]], axis=0)
        )
        right.append(
            jnp.where(jnp.broadcast_to(arrival[p : p + 1], (PER, ELEM)) == slot, 1.0, 0.0)
        )
    left = jnp.concatenate(left, axis=1).astype(jnp.bfloat16)
    right = jnp.concatenate(right, axis=1).astype(jnp.bfloat16)
    right = jnp.concatenate([right, right], axis=0)
    parts = lax.dot_general(
        left, right, (((1,), (1,)), ((), ())), preferred_element_type=jnp.float32
    )
    asked = (parts[:PEERS] * 256.0 + parts[PEERS:]).astype(jnp.int32)
    for r in range(PEERS):
        req_ref[r] = asked[r : r + 1]


def route(span_slot):
    return pl.pallas_call(
        route_kernel,
        out_shape=(
            pltpu.VMEM((PEERS, 1, ELEM), jnp.int32),
            pltpu.VMEM((PTS, ELEM), jnp.int32),
        ),
        in_specs=[VMEM],
        out_specs=(VMEM, VMEM),
        compiler_params=PARAMS,
        name="route",
    )(span_slot)


def reply_kernel(coef_ref, got_ref, out_ref, data):
    data[...] = parts_of(coef_ref[...])
    lane = iota((1, ELEM), 1)
    first_half = iota((8, ELEM), 1) < PER
    for pair in range(PTS // 2):
        chunks = (2 * pair, 2 * pair + 1)
        asked = [jnp.where(lane < PER, got_ref[2 * c], got_ref[2 * c + 1]) for c in chunks]
        value = moved(data[...], one_hot(jnp.concatenate(asked, axis=1), COLS))
        for u, c in enumerate(chunks):
            acc = [value[8 * b : 8 * b + 8, u * ELEM : (u + 1) * ELEM] for b in range(BLOCKS)]
            turned = [pltpu.roll(block, PER, 1) for block in acc]
            for b in range(5):
                upper = 5 + b if b < 4 else b
                at = slice(8 * b, 8 * b + 8)
                out_ref[2 * c, at, :] = jnp.where(first_half, acc[b], turned[upper])
                out_ref[2 * c + 1, at, :] = jnp.where(first_half, turned[b], acc[upper])


def reply(coef, got):
    return pl.pallas_call(
        reply_kernel,
        out_shape=pltpu.VMEM((PEERS, ROWS, ELEM), jnp.float32),
        in_specs=[VMEM, VMEM],
        out_specs=VMEM,
        scratch_shapes=[pltpu.VMEM((2 * LEV, COLS), jnp.bfloat16)],
        compiler_params=PARAMS,
        name="reply",
    )(inside(coef), inside(got))


TABLE = 5 * ELEM


def send_lanes(send_ref):
    lane = iota((1, ELEM), 1)
    chosen = jnp.full((1, ELEM), 4 * ELEM, jnp.int32)
    for i in range(2 * BC + 2 * BR):
        chosen = jnp.where(lane == i, send_ref[i], chosen)
    return chosen


def fill_edges(edges, point):
    for t in range(4):
        for s in range(4):
            edges[t * LEV : (t + 1) * LEV, s * ELEM : (s + 1) * ELEM] = point(EDGE_POINT[s][t])


def emit(edges, send_ref, row_ref, col_ref):
    out = moved(parts_of(edges[:, : 4 * ELEM]), one_hot(send_lanes(send_ref), 4 * ELEM))
    lane = iota((LEV, ELEM), 1)
    for t in range(4):
        here = out[t * LEV : (t + 1) * LEV]
        row = here if t == 0 else pltpu.roll(here, 32 * t, 1)
        col = pltpu.roll(here, ELEM - 32 + 16 * t, 1)
        row_out = row if t == 0 else jnp.where((lane >> 5) == t, row, row_out)
        col_out = col if t == 0 else jnp.where((lane >> 4) == t, col, col_out)
    row_ref[...] = row_out
    col_ref[...] = col_out


def halo_kernel(tracer_ref, send_ref, row_ref, col_ref, edges):
    fill_edges(edges, lambda p: tracer_ref[pl.ds(p, LEV, stride=PTS), :])
    emit(edges, send_ref, row_ref, col_ref)


FLAT = pltpu.VMEM((LEV, ELEM), jnp.float32)


def halo(tracer, send_slot):
    return pl.pallas_call(
        halo_kernel,
        out_shape=(FLAT, FLAT),
        in_specs=[VMEM, SMEM],
        out_specs=(VMEM, VMEM),
        scratch_shapes=[pltpu.VMEM((4 * LEV, 4 * ELEM), jnp.float32)],
        compiler_params=PARAMS,
        name="halo",
    )(inside(tracer), send_slot)


def gather_across(edges, across, nbr_ref, incoming):
    lane = iota((LEV, ELEM), 1)
    below, above, west, east = [ref[...] for ref in incoming]
    row_in = jnp.where((lane & 31) < BC, below, above)
    col_in = jnp.where((lane & 15) < BR, west, east)
    for t in range(4):
        row = row_in if t == 0 else pltpu.roll(row_in, ELEM - 32 * t, 1)
        col = pltpu.roll(col_in, 32 if t < 1 else (ELEM + 32 - 16 * t) % ELEM, 1) if t != 2 else col_in
        edges[t * LEV : (t + 1) * LEV, 4 * ELEM :] = jnp.where(lane < 32, row, col)
    index = jnp.concatenate([nbr_ref[s : s + 1, :] for s in range(4)], axis=1)
    across[...] = moved(parts_of(edges[...]), one_hot(index, TABLE))


def operator(slabs, metric, turned, across, b):
    stiff = stiffness()
    edge_sum = [None] * PTS
    for s in range(4):
        raw = [
            across[pl.ds(pl.multiple_of(t * LEV + b * 8, 8), 8), s * ELEM : (s + 1) * ELEM]
            for t in range(4)
        ]
        for t in range(4):
            p = EDGE_POINT[s][t]
            value = jnp.where(turned[s], raw[3 - t], raw[t])
            edge_sum[p] = value if edge_sum[p] is None else edge_sum[p] + value
    result = []
    for i in range(4):
        for j in range(4):
            p = 4 * i + j
            edges = (i in (0, 3)) + (j in (0, 3))
            total = slabs[p] * float(stiff[i, i] + stiff[j, j] - PENALTY * edges)
            for q in range(4):
                if q != i:
                    total = total + slabs[4 * q + j] * float(stiff[i, q])
                if q != j:
                    total = total + slabs[4 * i + q] * float(stiff[j, q])
            if edges:
                total = total + PENALTY * edge_sum[p]
            result.append(metric * total)
    return result


def turned_of(flip_ref):
    return [jnp.broadcast_to(flip_ref[s : s + 1, :], (8, ELEM)) == 1 for s in range(4)]


def first_kernel(
    tracer_ref, metric_ref, nbr_ref, flip_ref, send_ref, below_ref, above_ref, west_ref, east_ref,
    first_ref, row_ref, col_ref, edges, across,
):
    fill_edges(edges, lambda p: tracer_ref[pl.ds(p, LEV, stride=PTS), :])
    gather_across(edges, across, nbr_ref, (below_ref, above_ref, west_ref, east_ref))
    metric = jnp.broadcast_to(metric_ref[...], (8, ELEM))

    def block(b, carry):
        at = pl.ds(pl.multiple_of(b * 8, 8), 8)
        slabs = [tracer_ref[pl.ds(b * (8 * PTS) + p, 8, stride=PTS), :] for p in range(PTS)]
        result = operator(slabs, metric, turned_of(flip_ref), across, b)
        for p in range(PTS):
            first_ref[p, at, :] = result[p]
        return carry

    lax.fori_loop(0, BLOCKS, block, 0)
    fill_edges(edges, lambda p: first_ref[p])
    emit(edges, send_ref, row_ref, col_ref)


EDGE_SCRATCH = [
    pltpu.VMEM((4 * LEV, TABLE), jnp.float32),
    pltpu.VMEM((4 * LEV, 4 * ELEM), jnp.float32),
]


def first_pass(tracer, metric, nbr, flip, send_slot, incoming):
    return pl.pallas_call(
        first_kernel,
        out_shape=(pltpu.VMEM((PTS, LEV, ELEM), jnp.float32), FLAT, FLAT),
        in_specs=[VMEM, VMEM, VMEM, VMEM, SMEM] + [VMEM] * 4,
        out_specs=(VMEM, VMEM, VMEM),
        scratch_shapes=EDGE_SCRATCH,
        compiler_params=PARAMS,
        name="first_pass",
    )(inside(tracer), metric, nbr, flip, send_slot, *[inside(x) for x in incoming])


def second_kernel(
    tracer_ref, field_ref, metric_ref, nbr_ref, flip_ref, below_ref, above_ref, west_ref, east_ref,
    stepped_ref, edges, across,
):
    fill_edges(edges, lambda p: field_ref[p])
    gather_across(edges, across, nbr_ref, (below_ref, above_ref, west_ref, east_ref))
    metric = jnp.broadcast_to(metric_ref[...], (8, ELEM))

    def block(b, carry):
        at = pl.ds(pl.multiple_of(b * 8, 8), 8)
        slabs = [field_ref[p, at, :] for p in range(PTS)]
        result = operator(slabs, metric, turned_of(flip_ref), across, b)
        for p in range(PTS):
            point = pl.ds(b * (8 * PTS) + p, 8, stride=PTS)
            stepped_ref[point, :] = tracer_ref[point, :] - HYPER * result[p]
        return carry

    lax.fori_loop(0, BLOCKS, block, 0)


def second_pass(tracer, field, metric, nbr, flip, incoming):
    return pl.pallas_call(
        second_kernel,
        out_shape=pltpu.VMEM((LEV * PTS, ELEM), jnp.float32),
        in_specs=[VMEM] * 9,
        out_specs=VMEM,
        scratch_shapes=EDGE_SCRATCH,
        compiler_params=PARAMS,
        name="second_pass",
    )(inside(tracer), inside(field), metric, nbr, flip, *[inside(x) for x in incoming])


def mix_kernel(reply_ref, bucket_ref, stepped_ref, out_ref, wide, data, mixing, gain, carried):
    first_half = iota((8, ELEM), 1) < PER
    for c in range(PTS):
        lanes = slice(c * ELEM, (c + 1) * ELEM)
        even = [reply_ref[2 * c, 8 * b : 8 * b + 8, :] for b in range(5)]
        odd = [reply_ref[2 * c + 1, 8 * b : 8 * b + 8, :] for b in range(5)]
        for b in range(5):
            wide[8 * b : 8 * b + 8, lanes] = jnp.where(
                first_half, even[b], pltpu.roll(odd[b], PER, 1)
            )
        for b in range(4):
            wide[40 + 8 * b : 48 + 8 * b, lanes] = jnp.where(
                first_half, pltpu.roll(even[b], PER, 1), odd[b]
            )
    data[...] = parts_of(wide[...])
    for p in range(0, PTS, 2):
        index = jnp.concatenate([bucket_ref[p : p + 1, :], bucket_ref[p + 1 : p + 2, :]], axis=1)
        value = moved(data[...], one_hot(index, COLS))
        for u in range(2):
            mixing[pl.ds(p + u, LEV, stride=PTS), :] = value[:, u * ELEM : (u + 1) * ELEM]

    def level(ref, k):
        return ref[k * PTS : (k + 1) * PTS, :]

    zero = jnp.zeros((PTS, ELEM), jnp.float32)
    half = LEV // 2
    up_gain, up_rhs, down_gain, down_rhs = zero, zero, zero, zero
    for i in range(half):
        k = i
        here, after = level(mixing, k), level(mixing, k + 1)
        scale = 1.0 / (1.0 + after + here * (1.0 - up_gain))
        up_rhs = (level(stepped_ref, k) + here * up_rhs) * scale
        up_gain = after * scale
        if i < half - 1:
            gain[k * PTS : (k + 1) * PTS, :] = up_gain
            carried[k * PTS : (k + 1) * PTS, :] = up_rhs
        m = LEV - 1 - i
        here = level(mixing, m)
        after = zero if i == 0 else level(mixing, m + 1)
        scale = 1.0 / (1.0 + here + after * (1.0 - down_gain))
        down_rhs = (level(stepped_ref, m) + after * down_rhs) * scale
        down_gain = here * scale
        if i < half - 1:
            gain[m * PTS : (m + 1) * PTS, :] = down_gain
            carried[m * PTS : (m + 1) * PTS, :] = down_rhs
    upper = (up_rhs + up_gain * down_rhs) / (1.0 - up_gain * down_gain)
    lower = down_rhs + down_gain * upper
    out_ref[half - 1] = upper
    out_ref[half] = lower
    for i in range(half - 2, -1, -1):
        upper = level(carried, i) + level(gain, i) * upper
        out_ref[i] = upper
        m = LEV - 1 - i
        lower = level(carried, m) + level(gain, m) * lower
        out_ref[m] = lower


def mix(replied, bucket, stepped):
    rows = LEV * PTS
    return pl.pallas_call(
        mix_kernel,
        out_shape=jax.ShapeDtypeStruct((LEV, PTS, ELEM), jnp.float32),
        in_specs=[VMEM] * 3,
        out_specs=VMEM,
        scratch_shapes=[
            pltpu.VMEM((LEV, COLS), jnp.float32),
            pltpu.VMEM((2 * LEV, COLS), jnp.bfloat16),
            pltpu.VMEM((rows, ELEM), jnp.float32),
            pltpu.VMEM((rows, ELEM), jnp.float32),
            pltpu.VMEM((rows, ELEM), jnp.float32),
        ],
        compiler_params=PARAMS,
        name="mix",
    )(inside(replied), inside(bucket), inside(stepped))


def exchange(row_out, col_out):
    def both(value, axis):
        size = lax.axis_size(axis)
        up = [(i, (i + 1) % size) for i in range(size)]
        down = [(j, i) for i, j in up]
        return lax.ppermute(value, axis, up), lax.ppermute(value, axis, down)

    return both(row_out, "grp") + both(col_out, "dev")


def on_device(tracer, metric, coef, nbr_slot, edge_flip, send_slot, span_slot):
    flat = tracer.reshape(LEV * PTS, ELEM)
    metric = metric.reshape(1, ELEM)
    asked, bucket = route(span_slot)
    got = lax.all_to_all(asked, "dev", split_axis=0, concat_axis=0, tiled=True)
    row_out, col_out = halo(flat, send_slot)
    got, row_out, col_out = lax.optimization_barrier((got, row_out, col_out))
    incoming = exchange(row_out, col_out)
    replied = lax.all_to_all(reply(coef, got), "dev", split_axis=0, concat_axis=0, tiled=True)
    first, row_out, col_out = first_pass(flat, metric, nbr_slot, edge_flip, send_slot, incoming)
    stepped = second_pass(flat, first, metric, nbr_slot, edge_flip, exchange(row_out, col_out))
    return mix(replied, bucket, stepped)


def solution(mesh):
    in_specs = (
        P(None, None, ("grp", "dev")),
        P(("grp", "dev")),
        P(None, ("grp", "dev")),
        P(None, ("grp", "dev")),
        P(None, ("grp", "dev")),
        P(("grp", "dev")),
        P(None, ("grp", "dev")),
    )
    out_specs = P(None, None, ("grp", "dev"))
    return jax.shard_map(
        on_device, mesh=mesh, in_specs=in_specs, out_specs=out_specs, check_vma=False
    )
```

time: 325 us -> 73.5 us (0.23); the launches traced: 320 us -> 73 us
  local copies, waits for them, and re-layouts: 183 us -> 2.43 us
  waiting for transfers between devices: 47.8 us -> 15.2 us
  other arithmetic: 21.5 us -> 0 us
  Pallas kernels: 0 us -> 11.1 us
  starting transfers between devices: 54.4 us -> 44.1 us
  loops' own time: 6.86 us -> 0 us
  matrix products: 6.3 us -> 0 us
    dynamic_slice x216 -> x0, local copies, waits for them, and re-layouts: 67.1 us -> none  [vertical_solve(): lax.scan(forward, start, (sub_diag, diagonal, super_diag, values))]
    dynamic_update_slice x216 -> x0, local copies, waits for them, and re-layouts: 44.3 us -> none  [vertical_solve(): lax.scan(forward, start, (sub_diag, diagonal, super_diag, values))]
    all_to_all x3 -> x2, waiting for transfers between devices: 47.5 us -> 5.91 us  [the longest x1 5.91 us: on_device(): got = lax.all_to_all(asked, 'dev', split_axis=0, concat_axis=0, tiled=True)]
    gather x13 -> x0, local copies, waits for them, and re-layouts: 41.6 us -> none  [the longest x1 11.8 us: on_device(): sent_pos = jnp.take(target_pos, send_order)[None, :]]
    pallas_call x0 -> x6, Pallas kernels: none -> 11.1 us  [the longest x1 2.86 us: mix(): pl.pallas_call(mix_kernel, out_shape=jax.ShapeDtypeStruct((LEV, PTS, ELEM...]
    all_to_all x3 -> x2, starting transfers between devices: 27.5 us -> 18 us  [the longest x1 12.9 us: on_device(): got = lax.all_to_all(asked, 'dev', split_axis=0, concat_axis=0, tiled=True)]
    another operation x2 -> x0, other arithmetic: 9.27 us -> none
    ppermute x8, waiting for transfers between devices: 0.32 us -> 9.33 us  [both(): return (lax.ppermute(value, axis, up), lax.ppermute(value, axis, down))]
  transfers between devices with their start and end apart: 11 -> 10, of which waited for: 4 -> 4; matrix products, arithmetic and copies ran while one was open for 16% -> 0% of each run, Pallas kernels for 0% -> 6%
where the time goes in v1:
time: 73.5 us; the launch traced here: 73 us
  starting transfers between devices  44.1 us (60%)
  waiting for transfers between devices  15.2 us (21%)
  Pallas kernels  11.1 us (15%)
  local copies, waits for them, and re-layouts  2.43 us (3%)
    ppermute x8, starting transfers between devices, both(): return (lax.ppermute(value, axis, up), lax.ppermute(value, axis, down))  26.1 us
    all_to_all x1, starting transfers between devices, on_device(): got = lax.all_to_all(asked, 'dev', split_axis=0, concat_axis=0, tiled=True)  12.9 us
    ppermute x8, waiting for transfers between devices, both(): return (lax.ppermute(value, axis, up), lax.ppermute(value, axis, down))  9.33 us
    all_to_all x1, waiting for transfers between devices, on_device(): got = lax.all_to_all(asked, 'dev', split_axis=0, concat_axis=0, tiled=True)  5.91 us
    all_to_all x1, starting transfers between devices, on_device(): lax.all_to_all(reply(coef, got), 'dev', split_axis=0, concat_axis=0, tile...  5.09 us
    pallas_call x1, Pallas kernels, mix(): pl.pallas_call(mix_kernel, out_shape=jax.ShapeDtypeStruct((LEV, PTS, ELEM...  2.86 us
    pallas_call x1, Pallas kernels, first_pass(): pl.pallas_call(first_kernel, out_shape=(pltpu.VMEM((PTS, LEV, ELEM), jnp....  2.45 us
    unnamed x16, local copies, waits for them, and re-layouts  2.43 us
  transfers between devices with their start and end apart: 10, of which 4 were waited for; matrix products, arithmetic and copies ran while one was open for 0% of the time, Pallas kernels for 6%

profile of v1, /device:TPU:8, one launch (start us, length us, event | category | flops | bytes accessed | tf_op | source)
XLA Modules:
  0.0 73.0 jit_solution(6904385240702603279)
XLA Ops:
  0.0 0.7 copy-done.3
  0.7 1.2 %route.1 = (s32[32,1,128]{2,1,0:T(1,128)}, s32[16,128]{1,0:T(8,128)S(1)}) custom-call(s32[16,128]{1,0:T(8,128)S(1)} %copy-done.3), custom_call_target="tpu_custom_call" | custom-call | tf_op jit(solution)/shard_map/route/pallas_call | solution.py:125
  1.9 12.9 %all-to-all-start = ((s32[32,1,128]{2,1,0:T(1,128)}), s32[32,1,128]{2,1,0:T(1,128)S(1)}, u32[]{:S(2)}, u32[]{:S(2)}) async-start(s32[32,1,128]{2,1,0:T(1,128)} %get-tuple-element.15), calls=%async_computation | async-start | bytes 32768 | tf_op jit(solution)/shard_map/all_to_all | solution.py:425
  14.8 0.0 copy-start.7
  14.8 0.6 copy-done.7
  15.5 1.1 %copy-done = f32[72,16,128]{2,1,0:T(8,128)S(1)} copy-done((f32[72,16,128]{2,1,0:T(8,128)S(1)}, f32[72,16,128]{2,1,0:T(8,128)}, u32[]{:S(2)}) %copy-start) | copy-done | bytes 589848
  16.6 1.0 %halo.1 = (f32[72,128]{1,0:T(8,128)S(1)}, f32[72,128]{1,0:T(8,128)S(1)}) custom-call(f32[1152,128]{1,0:T(8,128)S(1)} %bitcast.2, s32[48]{0:T(128)S(1)} %copy-done.7), custom_call_target="tpu_custom_call" | custom-call | tf_op jit(solution)/shard_map/halo/pallas_call | solution.py:207
  17.6 5.9 %all-to-all-done.got_ref = s32[32,1,128]{2,1,0:T(1,128)S(1)} async-done(((s32[32,1,128]{2,1,0:T(1,128)}), s32[32,1,128]{2,1,0:T(1,128)S(1)}, u32[]{:S(2)}, u32[]{:S(2)}) %all-to-all-start) | async-done | bytes 16416 | tf_op jit(solution)/shard_map/all_to_all | solution.py:425
  23.5 2.4 %reply.1 = f32[32,40,128]{2,1,0:T(8,128)} custom-call(f32[72,2048]{1,0:T(8,128)S(1)} %copy-done.2, s32[32,1,128]{2,1,0:T(1,128)S(1)} %all-to-all-done.got_ref), custom_call_target="tpu_custom_call" | custom-call | tf_op jit(solution)/shard_map/reply/pallas_call | solution.py:157
  25.9 5.1 %all-to-all-start.1 = ((f32[32,40,128]{2,1,0:T(8,128)}), f32[32,40,128]{2,1,0:T(8,128)S(1)}, u32[]{:S(2)}, u32[]{:S(2)}) async-start(f32[32,40,128]{2,1,0:T(8,128)} %reply.1), calls=%async_computation.1 | async-start | bytes 1310720 | tf_op jit(solution)/shard_map/all_to_all | solution.py:429
  31.0 0.0 copy-start.6
  31.0 7.5 %collective-permute-start.1 = (f32[72,128]{1,0:T(8,128)S(1)}, f32[72,128]{1,0:T(8,128)S(1)}, u32[]{:S(2)}, u32[]{:S(2)}) collective-permute-start(f32[72,128]{1,0:T(8,128)S(1)} %get-tuple-element.20), channel_id=1, source_target_pairs={{32,0},{64,32},{96,64},{128,96},{160,128},{192,160},{224,192},{256... | collective-permute-start | bytes 110600 | tf_op jit(solution)/shard_map/ppermute | solution.py:416
  38.5 0.0 collective-permute-start
  38.5 2.5 %collective-permute-start.3 = (f32[72,128]{1,0:T(8,128)S(1)}, f32[72,128]{1,0:T(8,128)S(1)}, u32[]{:S(2)}, u32[]{:S(2)}) collective-permute-start(f32[72,128]{1,0:T(8,128)S(1)} %get-tuple-element.21), channel_id=1, source_target_pairs={{1,0},{2,1},{3,2},{4,3},{5,4},{6,5},{7,6},{8,7},{9,8},{10,9},{11,1... | collective-permute-start | bytes 110600 | tf_op jit(solution)/shard_map/ppermute | solution.py:416
  41.1 3.3 %collective-permute-start.2 = (f32[72,128]{1,0:T(8,128)S(1)}, f32[72,128]{1,0:T(8,128)S(1)}, u32[]{:S(2)}, u32[]{:S(2)}) collective-permute-start(f32[72,128]{1,0:T(8,128)S(1)} %get-tuple-element.21), channel_id=1, source_target_pairs={{0,1},{1,2},{2,3},{3,4},{4,5},{5,6},{6,7},{7,8},{8,9},{9,10},{10,1... | collective-permute-start | bytes 110600 | tf_op jit(solution)/shard_map/ppermute | solution.py:416
  44.4 0.0 collective-permute-done.1.above_ref
  44.4 0.0 collective-permute-done.below_ref
  44.4 0.2 collective-permute-done.3.east_ref
  44.6 5.2 %collective-permute-done.2.west_ref = f32[72,128]{1,0:T(8,128)S(1)} collective-permute-done((f32[72,128]{1,0:T(8,128)S(1)}, f32[72,128]{1,0:T(8,128)S(1)}, u32[]{:S(2)}, u32[]{:S(2)}) %collective-permute-start.2) | collective-permute-done | bytes 36896 | tf_op jit(solution)/shard_map/ppermute | solution.py:416
  49.8 0.0 copy-done.4
  49.9 2.4 %first_pass.1 = (f32[16,72,128]{2,1,0:T(8,128)S(1)}, f32[72,128]{1,0:T(8,128)S(1)}, f32[72,128]{1,0:T(8,128)S(1)}) custom-call(f32[1152,128]{1,0:T(8,128)S(1)} %bitcast.3, f32[1,128]{1,0:T(1,128)S(1)} %bitcast.5, s32[4,128]{1,0:T(4,128)S(1)} %copy-done.4, s32[4,128]{1,0:T(4,128)S(1)} %copy-done.5, s32[48]{0:T(128)S(1)} %copy-done.7, ...), custom_call_target="tpu_custom_call" | custom-call | tf_op jit(solution)/shard_map/first_pass/pallas_call | solution.py:292
  52.3 3.6 %collective-permute-start.5 = (f32[72,128]{1,0:T(8,128)S(1)}, f32[72,128]{1,0:T(8,128)S(1)}, u32[]{:S(2)}, u32[]{:S(2)}) collective-permute-start(f32[72,128]{1,0:T(8,128)S(1)} %get-tuple-element.23), channel_id=1, source_target_pairs={{32,0},{64,32},{96,64},{128,96},{160,128},{192,160},{224,192},{256... | collective-permute-start | bytes 110600 | tf_op jit(solution)/shard_map/ppermute | solution.py:416
  55.9 0.0 collective-permute-start.4
  55.9 7.2 %collective-permute-start.7 = (f32[72,128]{1,0:T(8,128)S(1)}, f32[72,128]{1,0:T(8,128)S(1)}, u32[]{:S(2)}, u32[]{:S(2)}) collective-permute-start(f32[72,128]{1,0:T(8,128)S(1)} %get-tuple-element.24), channel_id=1, source_target_pairs={{1,0},{2,1},{3,2},{4,3},{5,4},{6,5},{7,6},{8,7},{9,8},{10,9},{11,1... | collective-permute-start | bytes 110600 | tf_op jit(solution)/shard_map/ppermute | solution.py:416
  63.1 1.9 %collective-permute-start.6 = (f32[72,128]{1,0:T(8,128)S(1)}, f32[72,128]{1,0:T(8,128)S(1)}, u32[]{:S(2)}, u32[]{:S(2)}) collective-permute-start(f32[72,128]{1,0:T(8,128)S(1)} %get-tuple-element.24), channel_id=1, source_target_pairs={{0,1},{1,2},{2,3},{3,4},{4,5},{5,6},{6,7},{7,8},{8,9},{9,10},{10,1... | collective-permute-start | bytes 110600 | tf_op jit(solution)/shard_map/ppermute | solution.py:416
  65.1 0.0 collective-permute-done.5.above_ref
  65.1 0.0 collective-permute-done.4.below_ref
  65.1 0.0 collective-permute-done.7.east_ref
  65.1 3.9 %collective-permute-done.6.west_ref = f32[72,128]{1,0:T(8,128)S(1)} collective-permute-done((f32[72,128]{1,0:T(8,128)S(1)}, f32[72,128]{1,0:T(8,128)S(1)}, u32[]{:S(2)}, u32[]{:S(2)}) %collective-permute-start.6) | collective-permute-done | bytes 36896 | tf_op jit(solution)/shard_map/ppermute | solution.py:416
  69.0 1.2 %second_pass.1.stepped_ref = f32[1152,128]{1,0:T(8,128)S(1)} custom-call(f32[1152,128]{1,0:T(8,128)S(1)} %bitcast.4, f32[16,72,128]{2,1,0:T(8,128)S(1)} %get-tuple-element.22.field_ref, f32[1,128]{1,0:T(1,128)S(1)} %bitcast.6, s32[4,128]{1,0:T(4,128)S(1)} %copy-done.4, s32[4,128]{1,0:T(4,128)S(1)} %copy-done.5, ...), custom_call_target="tpu_custom_call" | custom-call | tf_op jit(solution)/shard_map/second_pass/pallas_call | solution.py:324
  70.2 0.0 all-to-all-done.1.reply_ref
  70.2 2.9 %mix.1 = f32[72,16,128]{2,1,0:T(8,128)} custom-call(f32[32,40,128]{2,1,0:T(8,128)S(1)} %all-to-all-done.1.reply_ref, s32[16,128]{1,0:T(8,128)S(1)} %get-tuple-element.19.bucket_ref, f32[1152,128]{1,0:T(8,128)S(1)} %second_pass.1.stepped_ref), custom_call_target="tpu_custom_call" | custom-call | tf_op jit(solution)/shard_map/mix/pallas_call | solution.py:394
  (10 shorter events, 0.0 us)
Async XLA Ops:
  0.0 0.7 copy-start.3
  1.9 21.6 %all-to-all-start = ((s32[32,1,128]{2,1,0:T(1,128)}), s32[32,1,128]{2,1,0:T(1,128)S(1)}, u32[]{:S(2)}, u32[]{:S(2)}) async-start(s32[32,1,128]{2,1,0:T(1,128)} %get-tuple-element.15), calls=%async_computation | async-start | bytes 32768 | tf_op jit(solution)/shard_map/all_to_all | solution.py:425
  14.8 0.7 copy-start.7
  15.5 1.1 %copy-start = (f32[72,16,128]{2,1,0:T(8,128)S(1)}, f32[72,16,128]{2,1,0:T(8,128)}, u32[]{:S(2)}) copy-start(f32[72,16,128]{2,1,0:T(8,128)} %param.7) | copy-start | bytes 1769476
  16.6 6.9 %copy-start.2 = (f32[72,2048]{1,0:T(8,128)S(1)}, f32[72,2048]{1,0:T(8,128)}, u32[]{:S(2)}) copy-start(f32[72,2048]{1,0:T(8,128)} %coef_ref.1) | copy-start | bytes 1769476
  25.9 23.9 %copy-start.1 = (f32[72,16,128]{2,1,0:T(8,128)S(1)}, f32[72,16,128]{2,1,0:T(8,128)}, u32[]{:S(2)}) copy-start(f32[72,16,128]{2,1,0:T(8,128)} %param.7) | copy-start | bytes 1769476
  25.9 23.9 %copy-start.4 = (s32[4,128]{1,0:T(4,128)S(1)}, s32[4,128]{1,0:T(4,128)}, u32[]{:S(2)}) copy-start(s32[4,128]{1,0:T(4,128)} %nbr_ref.3) | copy-start | bytes 6148
  25.9 23.9 %copy-start.5 = (s32[4,128]{1,0:T(4,128)S(1)}, s32[4,128]{1,0:T(4,128)}, u32[]{:S(2)}) copy-start(s32[4,128]{1,0:T(4,128)} %flip_ref.3) | copy-start | bytes 6148
  25.9 44.3 %all-to-all-start.1 = ((f32[32,40,128]{2,1,0:T(8,128)}), f32[32,40,128]{2,1,0:T(8,128)S(1)}, u32[]{:S(2)}, u32[]{:S(2)}) async-start(f32[32,40,128]{2,1,0:T(8,128)} %reply.1), calls=%async_computation.1 | async-start | bytes 1310720 | tf_op jit(solution)/shard_map/all_to_all | solution.py:429
  31.0 18.9 %copy-start.6 = (f32[128]{0:T(128)S(1)}, f32[128]{0:T(128)}, u32[]{:S(2)}) copy-start(f32[128]{0:T(128)} %param.8) | copy-start | bytes 1540
  31.0 13.4 %collective-permute-start.1 = (f32[72,128]{1,0:T(8,128)S(1)}, f32[72,128]{1,0:T(8,128)S(1)}, u32[]{:S(2)}, u32[]{:S(2)}) collective-permute-start(f32[72,128]{1,0:T(8,128)S(1)} %get-tuple-element.20), channel_id=1, source_target_pairs={{32,0},{64,32},{96,64},{128,96},{160,128},{192,160},{224,192},{256... | collective-permute-start | bytes 110600 | tf_op jit(solution)/shard_map/ppermute | solution.py:416
  38.5 5.9 %collective-permute-start = (f32[72,128]{1,0:T(8,128)S(1)}, f32[72,128]{1,0:T(8,128)S(1)}, u32[]{:S(2)}, u32[]{:S(2)}) collective-permute-start(f32[72,128]{1,0:T(8,128)S(1)} %get-tuple-element.20), channel_id=1, source_target_pairs={{0,32},{32,64},{64,96},{96,128},{128,160},{160,192},{192,224},{224... | collective-permute-start | bytes 110600 | tf_op jit(solution)/shard_map/ppermute | solution.py:416
  38.5 6.0 %collective-permute-start.3 = (f32[72,128]{1,0:T(8,128)S(1)}, f32[72,128]{1,0:T(8,128)S(1)}, u32[]{:S(2)}, u32[]{:S(2)}) collective-permute-start(f32[72,128]{1,0:T(8,128)S(1)} %get-tuple-element.21), channel_id=1, source_target_pairs={{1,0},{2,1},{3,2},{4,3},{5,4},{6,5},{7,6},{8,7},{9,8},{10,9},{11,1... | collective-permute-start | bytes 110600 | tf_op jit(solution)/shard_map/ppermute | solution.py:416
  41.1 8.8 %collective-permute-start.2 = (f32[72,128]{1,0:T(8,128)S(1)}, f32[72,128]{1,0:T(8,128)S(1)}, u32[]{:S(2)}, u32[]{:S(2)}) collective-permute-start(f32[72,128]{1,0:T(8,128)S(1)} %get-tuple-element.21), channel_id=1, source_target_pairs={{0,1},{1,2},{2,3},{3,4},{4,5},{5,6},{6,7},{7,8},{8,9},{9,10},{10,1... | collective-permute-start | bytes 110600 | tf_op jit(solution)/shard_map/ppermute | solution.py:416
  52.3 12.7 %collective-permute-start.5 = (f32[72,128]{1,0:T(8,128)S(1)}, f32[72,128]{1,0:T(8,128)S(1)}, u32[]{:S(2)}, u32[]{:S(2)}) collective-permute-start(f32[72,128]{1,0:T(8,128)S(1)} %get-tuple-element.23), channel_id=1, source_target_pairs={{32,0},{64,32},{96,64},{128,96},{160,128},{192,160},{224,192},{256... | collective-permute-start | bytes 110600 | tf_op jit(solution)/shard_map/ppermute | solution.py:416
  55.9 9.2 %collective-permute-start.4 = (f32[72,128]{1,0:T(8,128)S(1)}, f32[72,128]{1,0:T(8,128)S(1)}, u32[]{:S(2)}, u32[]{:S(2)}) collective-permute-start(f32[72,128]{1,0:T(8,128)S(1)} %get-tuple-element.23), channel_id=1, source_target_pairs={{0,32},{32,64},{64,96},{96,128},{128,160},{160,192},{192,224},{224... | collective-permute-start | bytes 110600 | tf_op jit(solution)/shard_map/ppermute | solution.py:416
  55.9 9.2 %collective-permute-start.7 = (f32[72,128]{1,0:T(8,128)S(1)}, f32[72,128]{1,0:T(8,128)S(1)}, u32[]{:S(2)}, u32[]{:S(2)}) collective-permute-start(f32[72,128]{1,0:T(8,128)S(1)} %get-tuple-element.24), channel_id=1, source_target_pairs={{1,0},{2,1},{3,2},{4,3},{5,4},{6,5},{7,6},{8,7},{9,8},{10,9},{11,1... | collective-permute-start | bytes 110600 | tf_op jit(solution)/shard_map/ppermute | solution.py:416
  63.1 5.9 %collective-permute-start.6 = (f32[72,128]{1,0:T(8,128)S(1)}, f32[72,128]{1,0:T(8,128)S(1)}, u32[]{:S(2)}, u32[]{:S(2)}) collective-permute-start(f32[72,128]{1,0:T(8,128)S(1)} %get-tuple-element.24), channel_id=1, source_target_pairs={{0,1},{1,2},{2,3},{3,4},{4,5},{5,6},{6,7},{7,8},{8,9},{9,10},{10,1... | collective-permute-start | bytes 110600 | tf_op jit(solution)/shard_map/ppermute | solution.py:416

commit v2 on v1

--- a/solution.py
+++ b/solution.py
@@ -14,14 +14,13 @@
 COLS = PTS * ELEM
 PEERS = 32
 PER = COLS // PEERS
-ROWS = 40
 BLOCKS = LEV // 8
+SCALE = 5
 
 PENALTY = 10.0
 HYPER = 0.0001
 
 VMEM = pl.BlockSpec(memory_space=pltpu.VMEM)
-SMEM = pl.BlockSpec(memory_space=pltpu.SMEM)
 PARAMS = pltpu.CompilerParams(vmem_limit_bytes=8 << 20)
 
 EDGE_POINT = [[0, 1, 2, 3], [3, 7, 11, 15], [12, 13, 14, 15], [0, 4, 8, 12]]
@@ -48,6 +47,10 @@
     return lax.broadcasted_iota(jnp.int32, shape, dim)
 
 
+def outside(value):
+    return pltpu.with_memory_space_constraint(value, pltpu.HBM)
+
+
 def parts_of(value):
     high = value.astype(jnp.bfloat16)
     low = (value - high.astype(jnp.float32)).astype(jnp.bfloat16)
@@ -74,11 +77,23 @@
     )
 
 
+def cost(micros):
+    work = int(SCALE * micros * 1e9)
+    return pl.CostEstimate(flops=work, bytes_accessed=1 << 20, transcendentals=0)
+
+
 def inside(value):
     return pltpu.with_memory_space_constraint(value, pltpu.VMEM)
 
 
-def route_kernel(span_ref, req_ref, bucket_ref):
+def route_kernel(
+    span_ref, nbr_ref, flip_ref, send_ref, metric_ref, req_ref, bucket_ref, table_ref, scale_ref
+):
+    table_ref[0:4, :] = nbr_ref[...]
+    table_ref[4:8, :] = flip_ref[...]
+    table_ref[8:16, :] = jnp.full((8, ELEM), 4 * ELEM, jnp.int32)
+    table_ref[8:9, : 2 * BC + 2 * BR] = send_ref[...]
+    scale_ref[...] = jnp.broadcast_to(metric_ref[...], (8, ELEM))
     span = span_ref[...]
     target = span >> 11
     pos = span & (COLS - 1)
@@ -121,20 +136,6 @@
         req_ref[r] = asked[r : r + 1]
 
 
-def route(span_slot):
-    return pl.pallas_call(
-        route_kernel,
-        out_shape=(
-            pltpu.VMEM((PEERS, 1, ELEM), jnp.int32),
-            pltpu.VMEM((PTS, ELEM), jnp.int32),
-        ),
-        in_specs=[VMEM],
-        out_specs=(VMEM, VMEM),
-        compiler_params=PARAMS,
-        name="route",
-    )(span_slot)
-
-
 def reply_kernel(coef_ref, got_ref, out_ref, data):
     data[...] = parts_of(coef_ref[...])
     lane = iota((1, ELEM), 1)
@@ -145,35 +146,28 @@
         value = moved(data[...], one_hot(jnp.concatenate(asked, axis=1), COLS))
         for u, c in enumerate(chunks):
             acc = [value[8 * b : 8 * b + 8, u * ELEM : (u + 1) * ELEM] for b in range(BLOCKS)]
-            turned = [pltpu.roll(block, PER, 1) for block in acc]
-            for b in range(5):
-                upper = 5 + b if b < 4 else b
-                at = slice(8 * b, 8 * b + 8)
-                out_ref[2 * c, at, :] = jnp.where(first_half, acc[b], turned[upper])
-                out_ref[2 * c + 1, at, :] = jnp.where(first_half, turned[b], acc[upper])
+            for b in range(BLOCKS):
+                turned = pltpu.roll(acc[b], PER, 1)
+                even = jnp.where(first_half, acc[b], pltpu.roll(turned, 4, 0))
+                odd = jnp.where(first_half, turned, pltpu.roll(acc[b], 4, 0))
+                out_ref[2 * c, b] = even[:4]
+                out_ref[2 * c + 1, b] = odd[:4]
 
 
 def reply(coef, got):
     return pl.pallas_call(
         reply_kernel,
-        out_shape=pltpu.VMEM((PEERS, ROWS, ELEM), jnp.float32),
+        out_shape=pltpu.VMEM((PEERS, BLOCKS, 4, ELEM), jnp.float32),
         in_specs=[VMEM, VMEM],
         out_specs=VMEM,
         scratch_shapes=[pltpu.VMEM((2 * LEV, COLS), jnp.bfloat16)],
         compiler_params=PARAMS,
+        cost_estimate=cost(2.4),
         name="reply",
     )(inside(coef), inside(got))
 
 
 TABLE = 5 * ELEM
-
-
-def send_lanes(send_ref):
-    lane = iota((1, ELEM), 1)
-    chosen = jnp.full((1, ELEM), 4 * ELEM, jnp.int32)
-    for i in range(2 * BC + 2 * BR):
-        chosen = jnp.where(lane == i, send_ref[i], chosen)
-    return chosen
 
 
 def fill_edges(edges, point):
@@ -182,8 +176,8 @@
             edges[t * LEV : (t + 1) * LEV, s * ELEM : (s + 1) * ELEM] = point(EDGE_POINT[s][t])
 
 
-def emit(edges, send_ref, row_ref, col_ref):
-    out = moved(parts_of(edges[:, : 4 * ELEM]), one_hot(send_lanes(send_ref), 4 * ELEM))
+def emit(edges, chosen, row_ref, col_ref):
+    out = moved(parts_of(edges[:, : 4 * ELEM]), one_hot(chosen, 4 * ELEM))
     lane = iota((LEV, ELEM), 1)
     for t in range(4):
         here = out[t * LEV : (t + 1) * LEV]
@@ -195,27 +189,45 @@
     col_ref[...] = col_out
 
 
-def halo_kernel(tracer_ref, send_ref, row_ref, col_ref, edges):
+FLAT = pltpu.VMEM((LEV, ELEM), jnp.float32)
+
+
+def route(span_slot, nbr_slot, edge_flip, send_slot, metric):
+    return pl.pallas_call(
+        route_kernel,
+        out_shape=(
+            pltpu.VMEM((PEERS, 1, ELEM), jnp.int32),
+            pltpu.VMEM((PTS, ELEM), jnp.int32),
+            pltpu.VMEM((16, ELEM), jnp.int32),
+            pltpu.VMEM((8, ELEM), jnp.float32),
+        ),
+        in_specs=[VMEM] * 5,
+        out_specs=(VMEM,) * 4,
+        compiler_params=PARAMS,
+        cost_estimate=cost(1.2),
+        name="route",
+    )(*[outside(x) for x in (span_slot, nbr_slot, edge_flip, send_slot.reshape(1, -1), metric.reshape(1, ELEM))])
+
+
+def halo_kernel(tracer_ref, table_ref, row_ref, col_ref, edges):
     fill_edges(edges, lambda p: tracer_ref[pl.ds(p, LEV, stride=PTS), :])
-    emit(edges, send_ref, row_ref, col_ref)
-
-
-FLAT = pltpu.VMEM((LEV, ELEM), jnp.float32)
-
-
-def halo(tracer, send_slot):
+    emit(edges, table_ref[8:9, :], row_ref, col_ref)
+
+
+def halo(tracer, table):
     return pl.pallas_call(
         halo_kernel,
         out_shape=(FLAT, FLAT),
-        in_specs=[VMEM, SMEM],
+        in_specs=[VMEM, VMEM],
         out_specs=(VMEM, VMEM),
         scratch_shapes=[pltpu.VMEM((4 * LEV, 4 * ELEM), jnp.float32)],
         compiler_params=PARAMS,
+        cost_estimate=cost(1.0),
         name="halo",
-    )(inside(tracer), send_slot)
-
-
-def gather_across(edges, across, nbr_ref, incoming):
+    )(inside(tracer), inside(table))
+
+
+def gather_across(edges, across, table_ref, incoming):
     lane = iota((LEV, ELEM), 1)
     below, above, west, east = [ref[...] for ref in incoming]
     row_in = jnp.where((lane & 31) < BC, below, above)
@@ -224,7 +236,7 @@
         row = row_in if t == 0 else pltpu.roll(row_in, ELEM - 32 * t, 1)
         col = pltpu.roll(col_in, 32 if t < 1 else (ELEM + 32 - 16 * t) % ELEM, 1) if t != 2 else col_in
         edges[t * LEV : (t + 1) * LEV, 4 * ELEM :] = jnp.where(lane < 32, row, col)
-    index = jnp.concatenate([nbr_ref[s : s + 1, :] for s in range(4)], axis=1)
+    index = jnp.concatenate([table_ref[s : s + 1, :] for s in range(4)], axis=1)
     across[...] = moved(parts_of(edges[...]), one_hot(index, TABLE))
 
 
@@ -257,29 +269,29 @@
     return result
 
 
-def turned_of(flip_ref):
-    return [jnp.broadcast_to(flip_ref[s : s + 1, :], (8, ELEM)) == 1 for s in range(4)]
+def turned_of(table_ref):
+    return [jnp.broadcast_to(table_ref[s : s + 1, :], (8, ELEM)) == 1 for s in range(4, 8)]
 
 
 def first_kernel(
-    tracer_ref, metric_ref, nbr_ref, flip_ref, send_ref, below_ref, above_ref, west_ref, east_ref,
+    tracer_ref, metric_ref, table_ref, below_ref, above_ref, west_ref, east_ref,
     first_ref, row_ref, col_ref, edges, across,
 ):
     fill_edges(edges, lambda p: tracer_ref[pl.ds(p, LEV, stride=PTS), :])
-    gather_across(edges, across, nbr_ref, (below_ref, above_ref, west_ref, east_ref))
-    metric = jnp.broadcast_to(metric_ref[...], (8, ELEM))
+    gather_across(edges, across, table_ref, (below_ref, above_ref, west_ref, east_ref))
+    metric = metric_ref[...]
 
     def block(b, carry):
         at = pl.ds(pl.multiple_of(b * 8, 8), 8)
         slabs = [tracer_ref[pl.ds(b * (8 * PTS) + p, 8, stride=PTS), :] for p in range(PTS)]
-        result = operator(slabs, metric, turned_of(flip_ref), across, b)
+        result = operator(slabs, metric, turned_of(table_ref), across, b)
         for p in range(PTS):
             first_ref[p, at, :] = result[p]
         return carry
 
     lax.fori_loop(0, BLOCKS, block, 0)
     fill_edges(edges, lambda p: first_ref[p])
-    emit(edges, send_ref, row_ref, col_ref)
+    emit(edges, table_ref[8:9, :], row_ref, col_ref)
 
 
 EDGE_SCRATCH = [
@@ -288,30 +300,31 @@
 ]
 
 
-def first_pass(tracer, metric, nbr, flip, send_slot, incoming):
+def first_pass(tracer, metric, table, incoming):
     return pl.pallas_call(
         first_kernel,
         out_shape=(pltpu.VMEM((PTS, LEV, ELEM), jnp.float32), FLAT, FLAT),
-        in_specs=[VMEM, VMEM, VMEM, VMEM, SMEM] + [VMEM] * 4,
+        in_specs=[VMEM] * 7,
         out_specs=(VMEM, VMEM, VMEM),
         scratch_shapes=EDGE_SCRATCH,
         compiler_params=PARAMS,
+        cost_estimate=cost(2.4),
         name="first_pass",
-    )(inside(tracer), metric, nbr, flip, send_slot, *[inside(x) for x in incoming])
+    )(*[inside(x) for x in (tracer, metric, table, *incoming)])
 
 
 def second_kernel(
-    tracer_ref, field_ref, metric_ref, nbr_ref, flip_ref, below_ref, above_ref, west_ref, east_ref,
+    tracer_ref, field_ref, metric_ref, table_ref, below_ref, above_ref, west_ref, east_ref,
     stepped_ref, edges, across,
 ):
     fill_edges(edges, lambda p: field_ref[p])
-    gather_across(edges, across, nbr_ref, (below_ref, above_ref, west_ref, east_ref))
-    metric = jnp.broadcast_to(metric_ref[...], (8, ELEM))
+    gather_across(edges, across, table_ref, (below_ref, above_ref, west_ref, east_ref))
+    metric = metric_ref[...]
 
     def block(b, carry):
         at = pl.ds(pl.multiple_of(b * 8, 8), 8)
         slabs = [field_ref[p, at, :] for p in range(PTS)]
-        result = operator(slabs, metric, turned_of(flip_ref), across, b)
+        result = operator(slabs, metric, turned_of(table_ref), across, b)
         for p in range(PTS):
             point = pl.ds(b * (8 * PTS) + p, 8, stride=PTS)
             stepped_ref[point, :] = tracer_ref[point, :] - HYPER * result[p]
@@ -320,32 +333,28 @@
     lax.fori_loop(0, BLOCKS, block, 0)
 
 
-def second_pass(tracer, field, metric, nbr, flip, incoming):
+def second_pass(tracer, field, metric, table, incoming):
     return pl.pallas_call(
         second_kernel,
         out_shape=pltpu.VMEM((LEV * PTS, ELEM), jnp.float32),
-        in_specs=[VMEM] * 9,
+        in_specs=[VMEM] * 8,
         out_specs=VMEM,
         scratch_shapes=EDGE_SCRATCH,
         compiler_params=PARAMS,
+        cost_estimate=cost(1.2),
         name="second_pass",
-    )(inside(tracer), inside(field), metric, nbr, flip, *[inside(x) for x in incoming])
+    )(*[inside(x) for x in (tracer, field, metric, table, *incoming)])
 
 
 def mix_kernel(reply_ref, bucket_ref, stepped_ref, out_ref, wide, data, mixing, gain, carried):
-    first_half = iota((8, ELEM), 1) < PER
+    first_half = iota((4, ELEM), 1) < PER
     for c in range(PTS):
         lanes = slice(c * ELEM, (c + 1) * ELEM)
-        even = [reply_ref[2 * c, 8 * b : 8 * b + 8, :] for b in range(5)]
-        odd = [reply_ref[2 * c + 1, 8 * b : 8 * b + 8, :] for b in range(5)]
-        for b in range(5):
-            wide[8 * b : 8 * b + 8, lanes] = jnp.where(
-                first_half, even[b], pltpu.roll(odd[b], PER, 1)
-            )
-        for b in range(4):
-            wide[40 + 8 * b : 48 + 8 * b, lanes] = jnp.where(
-                first_half, pltpu.roll(even[b], PER, 1), odd[b]
-            )
+        for b in range(BLOCKS):
+            even, odd = reply_ref[2 * c, b], reply_ref[2 * c + 1, b]
+            low = jnp.where(first_half, even, pltpu.roll(odd, PER, 1))
+            high = jnp.where(first_half, pltpu.roll(even, PER, 1), odd)
+            wide[8 * b : 8 * b + 8, lanes] = jnp.concatenate([low, high], axis=0)
     data[...] = parts_of(wide[...])
     for p in range(0, PTS, 2):
         index = jnp.concatenate([bucket_ref[p : p + 1, :], bucket_ref[p + 1 : p + 2, :]], axis=1)
@@ -404,6 +413,7 @@
             pltpu.VMEM((rows, ELEM), jnp.float32),
         ],
         compiler_params=PARAMS,
+        cost_estimate=cost(2.8),
         name="mix",
     )(inside(replied), inside(bucket), inside(stepped))
 
@@ -420,15 +430,13 @@
 
 def on_device(tracer, metric, coef, nbr_slot, edge_flip, send_slot, span_slot):
     flat = tracer.reshape(LEV * PTS, ELEM)
-    metric = metric.reshape(1, ELEM)
-    asked, bucket = route(span_slot)
+    asked, bucket, table, metric = route(span_slot, nbr_slot, edge_flip, send_slot, metric)
+    row_out, col_out = halo(flat, table)
     got = lax.all_to_all(asked, "dev", split_axis=0, concat_axis=0, tiled=True)
-    row_out, col_out = halo(flat, send_slot)
-    got, row_out, col_out = lax.optimization_barrier((got, row_out, col_out))
     incoming = exchange(row_out, col_out)
     replied = lax.all_to_all(reply(coef, got), "dev", split_axis=0, concat_axis=0, tiled=True)
-    first, row_out, col_out = first_pass(flat, metric, nbr_slot, edge_flip, send_slot, incoming)
-    stepped = second_pass(flat, first, metric, nbr_slot, edge_flip, exchange(row_out, col_out))
+    first, row_out, col_out = first_pass(flat, metric, table, incoming)
+    stepped = second_pass(flat, first, metric, table, exchange(row_out, col_out))
     return mix(replied, bucket, stepped)
 
 

time: 73.5 us -> 65.2 us (0.89)
  the two profiles are of different devices: /device:TPU:8 before, /device:TPU:1 now
where the time goes in v2:
time: 65.2 us; the launch traced here: 64.8 us
  starting transfers between devices  47.8 us (73%)
  Pallas kernels  10.8 us (17%)
  waiting for transfers between devices  6.09 us (9%)
    ppermute x8, starting transfers between devices, both(): return (lax.ppermute(value, axis, up), lax.ppermute(value, axis, down))  30.9 us
    all_to_all x1, starting transfers between devices, on_device(): got = lax.all_to_all(asked, 'dev', split_axis=0, concat_axis=0, tiled=True)  10.5 us
    all_to_all x1, starting transfers between devices, on_device(): lax.all_to_all(reply(coef, got), 'dev', split_axis=0, concat_axis=0, tile...  6.45 us
    ppermute x8, waiting for transfers between devices, both(): return (lax.ppermute(value, axis, up), lax.ppermute(value, axis, down))  6.08 us
    pallas_call x1, Pallas kernels, mix(): pl.pallas_call(mix_kernel, out_shape=jax.ShapeDtypeStruct((LEV, PTS, ELEM...  2.92 us
    pallas_call x1, Pallas kernels, reply(): pl.pallas_call(reply_kernel, out_shape=pltpu.VMEM((PEERS, BLOCKS, 4, ELEM...  2.35 us
    pallas_call x1, Pallas kernels, route(): pl.pallas_call(route_kernel, out_shape=(pltpu.VMEM((PEERS, 1, ELEM), jnp....  1.98 us
    pallas_call x1, Pallas kernels, first_pass(): pl.pallas_call(first_kernel, out_shape=(pltpu.VMEM((PTS, LEV, ELEM), jnp....  1.88 us
  transfers between devices with their start and end apart: 10, of which 1 were waited for; matrix products, arithmetic and copies ran while one was open for 0% of the time, Pallas kernels for 9%

profile of v2, /device:TPU:1, one launch (start us, length us, event | category | flops | bytes accessed | tf_op | source)
XLA Modules:
  0.0 64.8 jit_solution(16640327274865161306)
XLA Ops:
  0.0 0.0 copy-start.1
  0.0 2.0 %route.1 = (s32[32,1,128]{2,1,0:T(1,128)}, s32[16,128]{1,0:T(8,128)S(1)}, s32[16,128]{1,0:T(8,128)S(1)}, f32[8,128]{1,0:T(8,128)S(1)}) custom-call(s32[16,128]{1,0:T(8,128)} %span_ref.1, s32[4,128]{1,0:T(4,128)} %nbr_ref.1, s32[4,128]{1,0:T(4,128)} %flip_ref.1, s32[1,48]{1,0:T(1,128)} %bitcast.6, f32[1,128]{1,0:T(1,128)} %bitcast.7), custom_call_target="tpu_custom_call" | custom-call | flops 6000000000 | bytes 1048576 | tf_op jit(solution)/shard_map/route/pallas_call | solution.py:196
  2.0 10.5 %all-to-all-start = ((s32[32,1,128]{2,1,0:T(1,128)}), s32[32,1,128]{2,1,0:T(1,128)S(1)}, u32[]{:S(2)}, u32[]{:S(2)}) async-start(s32[32,1,128]{2,1,0:T(1,128)} %get-tuple-element.14), calls=%async_computation | async-start | bytes 32768 | tf_op jit(solution)/shard_map/all_to_all | solution.py:435
  12.5 0.0 copy-done.1
  12.5 0.0 copy-start
  12.5 0.5 halo.1
  13.0 3.9 %collective-permute-start.1 = (f32[72,128]{1,0:T(8,128)S(1)}, f32[72,128]{1,0:T(8,128)S(1)}, u32[]{:S(2)}, u32[]{:S(2)}) collective-permute-start(f32[72,128]{1,0:T(8,128)S(1)} %get-tuple-element.18), channel_id=1, source_target_pairs={{32,0},{64,32},{96,64},{128,96},{160,128},{192,160},{224,192},{256... | collective-permute-start | bytes 110600 | tf_op jit(solution)/shard_map/ppermute | solution.py:426
  16.8 0.0 collective-permute-start
  16.8 6.8 %collective-permute-start.3 = (f32[72,128]{1,0:T(8,128)S(1)}, f32[72,128]{1,0:T(8,128)S(1)}, u32[]{:S(2)}, u32[]{:S(2)}) collective-permute-start(f32[72,128]{1,0:T(8,128)S(1)} %get-tuple-element.19), channel_id=1, source_target_pairs={{1,0},{2,1},{3,2},{4,3},{5,4},{6,5},{7,6},{8,7},{9,8},{10,9},{11,1... | collective-permute-start | bytes 110600 | tf_op jit(solution)/shard_map/ppermute | solution.py:426
  23.7 1.9 %collective-permute-start.2 = (f32[72,128]{1,0:T(8,128)S(1)}, f32[72,128]{1,0:T(8,128)S(1)}, u32[]{:S(2)}, u32[]{:S(2)}) collective-permute-start(f32[72,128]{1,0:T(8,128)S(1)} %get-tuple-element.19), channel_id=1, source_target_pairs={{0,1},{1,2},{2,3},{3,4},{4,5},{5,6},{6,7},{7,8},{8,9},{9,10},{10,1... | collective-permute-start | bytes 110600 | tf_op jit(solution)/shard_map/ppermute | solution.py:426
  25.6 0.0 all-to-all-done.got_ref
  25.6 0.0 copy-done
  25.6 2.3 %reply.1 = f32[32,9,4,128]{3,2,1,0:T(4,128)} custom-call(f32[72,2048]{1,0:T(8,128)S(1)} %copy-done, s32[32,1,128]{2,1,0:T(1,128)S(1)} %all-to-all-done.got_ref), custom_call_target="tpu_custom_call" | custom-call | flops 12000000000 | bytes 1048576 | tf_op jit(solution)/shard_map/reply/pallas_call | solution.py:158
  28.0 6.4 %all-to-all-start.1 = ((f32[32,9,4,128]{3,2,1,0:T(4,128)}), f32[32,9,4,128]{3,2,1,0:T(4,128)S(1)}, u32[]{:S(2)}, u32[]{:S(2)}) async-start(f32[32,9,4,128]{3,2,1,0:T(4,128)} %reply.1), calls=%async_computation.1 | async-start | bytes 1179648 | tf_op jit(solution)/shard_map/all_to_all | solution.py:437
  34.4 0.0 collective-permute-done.1.above_ref
  34.4 0.0 collective-permute-done.below_ref
  34.4 0.0 collective-permute-done.3.east_ref
  34.5 0.0 collective-permute-done.2.west_ref
  34.5 1.9 %first_pass.1 = (f32[16,72,128]{2,1,0:T(8,128)S(1)}, f32[72,128]{1,0:T(8,128)S(1)}, f32[72,128]{1,0:T(8,128)S(1)}) custom-call(f32[1152,128]{1,0:T(8,128)S(1)} %bitcast.4, f32[8,128]{1,0:T(8,128)S(1)} %get-tuple-element.16.metric_ref, s32[16,128]{1,0:T(8,128)S(1)} %get-tuple-element.17.table_ref, f32[72,128]{1,0:T(8,128)S(1)} %collective-permute-done.below_ref, ...), custom_call_target="tpu_custom_call" | custom-call | flops 12000000000 | bytes 1048576 | tf_op jit(solution)/shard_map/first_pass/pallas_call | solution.py:304
  36.4 9.5 %collective-permute-start.5 = (f32[72,128]{1,0:T(8,128)S(1)}, f32[72,128]{1,0:T(8,128)S(1)}, u32[]{:S(2)}, u32[]{:S(2)}) collective-permute-start(f32[72,128]{1,0:T(8,128)S(1)} %get-tuple-element.21), channel_id=1, source_target_pairs={{32,0},{64,32},{96,64},{128,96},{160,128},{192,160},{224,192},{256... | collective-permute-start | bytes 110600 | tf_op jit(solution)/shard_map/ppermute | solution.py:426
  45.9 0.0 collective-permute-start.4
  45.9 6.8 %collective-permute-start.7 = (f32[72,128]{1,0:T(8,128)S(1)}, f32[72,128]{1,0:T(8,128)S(1)}, u32[]{:S(2)}, u32[]{:S(2)}) collective-permute-start(f32[72,128]{1,0:T(8,128)S(1)} %get-tuple-element.22), channel_id=1, source_target_pairs={{1,0},{2,1},{3,2},{4,3},{5,4},{6,5},{7,6},{8,7},{9,8},{10,9},{11,1... | collective-permute-start | bytes 110600 | tf_op jit(solution)/shard_map/ppermute | solution.py:426
  52.7 1.9 %collective-permute-start.6 = (f32[72,128]{1,0:T(8,128)S(1)}, f32[72,128]{1,0:T(8,128)S(1)}, u32[]{:S(2)}, u32[]{:S(2)}) collective-permute-start(f32[72,128]{1,0:T(8,128)S(1)} %get-tuple-element.22), channel_id=1, source_target_pairs={{0,1},{1,2},{2,3},{3,4},{4,5},{5,6},{6,7},{7,8},{8,9},{9,10},{10,1... | collective-permute-start | bytes 110600 | tf_op jit(solution)/shard_map/ppermute | solution.py:426
  54.6 0.0 collective-permute-done.5.above_ref
  54.6 0.0 collective-permute-done.4.below_ref
  54.6 0.0 collective-permute-done.7.east_ref
  54.7 6.1 %collective-permute-done.6.west_ref = f32[72,128]{1,0:T(8,128)S(1)} collective-permute-done((f32[72,128]{1,0:T(8,128)S(1)}, f32[72,128]{1,0:T(8,128)S(1)}, u32[]{:S(2)}, u32[]{:S(2)}) %collective-permute-start.6) | collective-permute-done | bytes 36896 | tf_op jit(solution)/shard_map/ppermute | solution.py:426
  60.7 1.2 %second_pass.1.stepped_ref = f32[1152,128]{1,0:T(8,128)S(1)} custom-call(f32[1152,128]{1,0:T(8,128)S(1)} %bitcast.5, f32[16,72,128]{2,1,0:T(8,128)S(1)} %get-tuple-element.20.field_ref, f32[8,128]{1,0:T(8,128)S(1)} %get-tuple-element.16.metric_ref, s32[16,128]{1,0:T(8,128)S(1)} %get-tuple-element.17.table_ref, ...), custom_call_target="tpu_custom_call" | custom-call | flops 6000000000 | bytes 1048576 | tf_op jit(solution)/shard_map/second_pass/pallas_call | solution.py:337
  61.9 0.0 all-to-all-done.1.reply_ref
  61.9 2.9 %mix.1 = f32[72,16,128]{2,1,0:T(8,128)} custom-call(f32[32,9,4,128]{3,2,1,0:T(4,128)S(1)} %all-to-all-done.1.reply_ref, s32[16,128]{1,0:T(8,128)S(1)} %get-tuple-element.15.bucket_ref, f32[1152,128]{1,0:T(8,128)S(1)} %second_pass.1.stepped_ref), custom_call_target="tpu_custom_call" | custom-call | flops 14000000000 | bytes 1048576 | tf_op jit(solution)/shard_map/mix/pallas_call | solution.py:403
Async XLA Ops:
  0.0 12.5 %copy-start.1 = (f32[72,16,128]{2,1,0:T(8,128)S(1)}, f32[72,16,128]{2,1,0:T(8,128)}, u32[]{:S(2)}) copy-start(f32[72,16,128]{2,1,0:T(8,128)} %param.7) | copy-start | bytes 1769476
  2.0 23.6 %all-to-all-start = ((s32[32,1,128]{2,1,0:T(1,128)}), s32[32,1,128]{2,1,0:T(1,128)S(1)}, u32[]{:S(2)}, u32[]{:S(2)}) async-start(s32[32,1,128]{2,1,0:T(1,128)} %get-tuple-element.14), calls=%async_computation | async-start | bytes 32768 | tf_op jit(solution)/shard_map/all_to_all | solution.py:435
  12.5 13.1 %copy-start = (f32[72,2048]{1,0:T(8,128)S(1)}, f32[72,2048]{1,0:T(8,128)}, u32[]{:S(2)}) copy-start(f32[72,2048]{1,0:T(8,128)} %coef_ref.1) | copy-start | bytes 1769476
  13.0 21.4 %collective-permute-start.1 = (f32[72,128]{1,0:T(8,128)S(1)}, f32[72,128]{1,0:T(8,128)S(1)}, u32[]{:S(2)}, u32[]{:S(2)}) collective-permute-start(f32[72,128]{1,0:T(8,128)S(1)} %get-tuple-element.18), channel_id=1, source_target_pairs={{32,0},{64,32},{96,64},{128,96},{160,128},{192,160},{224,192},{256... | collective-permute-start | bytes 110600 | tf_op jit(solution)/shard_map/ppermute | solution.py:426
  16.8 17.6 %collective-permute-start = (f32[72,128]{1,0:T(8,128)S(1)}, f32[72,128]{1,0:T(8,128)S(1)}, u32[]{:S(2)}, u32[]{:S(2)}) collective-permute-start(f32[72,128]{1,0:T(8,128)S(1)} %get-tuple-element.18), channel_id=1, source_target_pairs={{0,32},{32,64},{64,96},{96,128},{128,160},{160,192},{192,224},{224... | collective-permute-start | bytes 110600 | tf_op jit(solution)/shard_map/ppermute | solution.py:426
  16.8 17.6 %collective-permute-start.3 = (f32[72,128]{1,0:T(8,128)S(1)}, f32[72,128]{1,0:T(8,128)S(1)}, u32[]{:S(2)}, u32[]{:S(2)}) collective-permute-start(f32[72,128]{1,0:T(8,128)S(1)} %get-tuple-element.19), channel_id=1, source_target_pairs={{1,0},{2,1},{3,2},{4,3},{5,4},{6,5},{7,6},{8,7},{9,8},{10,9},{11,1... | collective-permute-start | bytes 110600 | tf_op jit(solution)/shard_map/ppermute | solution.py:426
  23.7 10.8 %collective-permute-start.2 = (f32[72,128]{1,0:T(8,128)S(1)}, f32[72,128]{1,0:T(8,128)S(1)}, u32[]{:S(2)}, u32[]{:S(2)}) collective-permute-start(f32[72,128]{1,0:T(8,128)S(1)} %get-tuple-element.19), channel_id=1, source_target_pairs={{0,1},{1,2},{2,3},{3,4},{4,5},{5,6},{6,7},{7,8},{8,9},{9,10},{10,1... | collective-permute-start | bytes 110600 | tf_op jit(solution)/shard_map/ppermute | solution.py:426
  28.0 33.9 %all-to-all-start.1 = ((f32[32,9,4,128]{3,2,1,0:T(4,128)}), f32[32,9,4,128]{3,2,1,0:T(4,128)S(1)}, u32[]{:S(2)}, u32[]{:S(2)}) async-start(f32[32,9,4,128]{3,2,1,0:T(4,128)} %reply.1), calls=%async_computation.1 | async-start | bytes 1179648 | tf_op jit(solution)/shard_map/all_to_all | solution.py:437
  36.4 18.3 %collective-permute-start.5 = (f32[72,128]{1,0:T(8,128)S(1)}, f32[72,128]{1,0:T(8,128)S(1)}, u32[]{:S(2)}, u32[]{:S(2)}) collective-permute-start(f32[72,128]{1,0:T(8,128)S(1)} %get-tuple-element.21), channel_id=1, source_target_pairs={{32,0},{64,32},{96,64},{128,96},{160,128},{192,160},{224,192},{256... | collective-permute-start | bytes 110600 | tf_op jit(solution)/shard_map/ppermute | solution.py:426
  45.9 8.8 %collective-permute-start.4 = (f32[72,128]{1,0:T(8,128)S(1)}, f32[72,128]{1,0:T(8,128)S(1)}, u32[]{:S(2)}, u32[]{:S(2)}) collective-permute-start(f32[72,128]{1,0:T(8,128)S(1)} %get-tuple-element.21), channel_id=1, source_target_pairs={{0,32},{32,64},{64,96},{96,128},{128,160},{160,192},{192,224},{224... | collective-permute-start | bytes 110600 | tf_op jit(solution)/shard_map/ppermute | solution.py:426
  45.9 8.8 %collective-permute-start.7 = (f32[72,128]{1,0:T(8,128)S(1)}, f32[72,128]{1,0:T(8,128)S(1)}, u32[]{:S(2)}, u32[]{:S(2)}) collective-permute-start(f32[72,128]{1,0:T(8,128)S(1)} %get-tuple-element.22), channel_id=1, source_target_pairs={{1,0},{2,1},{3,2},{4,3},{5,4},{6,5},{7,6},{8,7},{9,8},{10,9},{11,1... | collective-permute-start | bytes 110600 | tf_op jit(solution)/shard_map/ppermute | solution.py:426
  52.7 8.0 %collective-permute-start.6 = (f32[72,128]{1,0:T(8,128)S(1)}, f32[72,128]{1,0:T(8,128)S(1)}, u32[]{:S(2)}, u32[]{:S(2)}) collective-permute-start(f32[72,128]{1,0:T(8,128)S(1)} %get-tuple-element.22), channel_id=1, source_target_pairs={{0,1},{1,2},{2,3},{3,4},{4,5},{5,6},{6,7},{7,8},{8,9},{9,10},{10,1... | collective-permute-start | bytes 110600 | tf_op jit(solution)/shard_map/ppermute | solution.py:426

commit v3 on v2

--- a/solution.py
+++ b/solution.py
@@ -176,20 +176,34 @@
             edges[t * LEV : (t + 1) * LEV, s * ELEM : (s + 1) * ELEM] = point(EDGE_POINT[s][t])
 
 
-def emit(edges, chosen, row_ref, col_ref):
+def turn(value, lanes):
+    lanes = lanes % ELEM
+    return pltpu.roll(value, lanes, 1) if lanes else value
+
+
+def emit(edges, chosen, row_ref, east_ref, west_ref):
     out = moved(parts_of(edges[:, : 4 * ELEM]), one_hot(chosen, 4 * ELEM))
+    out = [out[t * LEV : (t + 1) * LEV] for t in range(4)]
     lane = iota((LEV, ELEM), 1)
-    for t in range(4):
-        here = out[t * LEV : (t + 1) * LEV]
-        row = here if t == 0 else pltpu.roll(here, 32 * t, 1)
-        col = pltpu.roll(here, ELEM - 32 + 16 * t, 1)
-        row_out = row if t == 0 else jnp.where((lane >> 5) == t, row, row_out)
-        col_out = col if t == 0 else jnp.where((lane >> 4) == t, col, col_out)
-    row_ref[...] = row_out
-    col_ref[...] = col_out
-
-
+    value = out[0]
+    for t in range(1, 4):
+        value = jnp.where((lane >> 5) == t, turn(out[t], 32 * t), value)
+    row_ref[...] = value
+    lane24 = iota((THIRD, ELEM), 1)
+    for start, ref in ((2 * BC, east_ref), (2 * BC + BR, west_ref)):
+        value = turn(out[0], -start)
+        for t in range(1, 4):
+            value = jnp.where((lane >> 3) == t, turn(out[t], 8 * t - start), value)
+        packed = value[:THIRD]
+        for j in range(1, 3):
+            block = turn(value[j * THIRD : (j + 1) * THIRD], 32 * j)
+            packed = jnp.where((lane24 >> 5) == j, block, packed)
+        ref[...] = packed
+
+
+THIRD = LEV // 3
 FLAT = pltpu.VMEM((LEV, ELEM), jnp.float32)
+SIDE = pltpu.VMEM((THIRD, ELEM), jnp.float32)
 
 
 def route(span_slot, nbr_slot, edge_flip, send_slot, metric):
@@ -209,17 +223,17 @@
     )(*[outside(x) for x in (span_slot, nbr_slot, edge_flip, send_slot.reshape(1, -1), metric.reshape(1, ELEM))])
 
 
-def halo_kernel(tracer_ref, table_ref, row_ref, col_ref, edges):
+def halo_kernel(tracer_ref, table_ref, row_ref, east_ref, west_ref, edges):
     fill_edges(edges, lambda p: tracer_ref[pl.ds(p, LEV, stride=PTS), :])
-    emit(edges, table_ref[8:9, :], row_ref, col_ref)
+    emit(edges, table_ref[8:9, :], row_ref, east_ref, west_ref)
 
 
 def halo(tracer, table):
     return pl.pallas_call(
         halo_kernel,
-        out_shape=(FLAT, FLAT),
+        out_shape=(FLAT, SIDE, SIDE),
         in_specs=[VMEM, VMEM],
-        out_specs=(VMEM, VMEM),
+        out_specs=(VMEM,) * 3,
         scratch_shapes=[pltpu.VMEM((4 * LEV, 4 * ELEM), jnp.float32)],
         compiler_params=PARAMS,
         cost_estimate=cost(1.0),
@@ -227,22 +241,32 @@
     )(inside(tracer), inside(table))
 
 
-def gather_across(edges, across, table_ref, incoming):
+def received(incoming):
+    below, above, west, east = [ref[...] for ref in incoming]
     lane = iota((LEV, ELEM), 1)
-    below, above, west, east = [ref[...] for ref in incoming]
+    lane24 = iota((THIRD, ELEM), 1)
     row_in = jnp.where((lane & 31) < BC, below, above)
-    col_in = jnp.where((lane & 15) < BR, west, east)
+    result = []
     for t in range(4):
-        row = row_in if t == 0 else pltpu.roll(row_in, ELEM - 32 * t, 1)
-        col = pltpu.roll(col_in, 32 if t < 1 else (ELEM + 32 - 16 * t) % ELEM, 1) if t != 2 else col_in
-        edges[t * LEV : (t + 1) * LEV, 4 * ELEM :] = jnp.where(lane < 32, row, col)
-    index = jnp.concatenate([table_ref[s : s + 1, :] for s in range(4)], axis=1)
-    across[...] = moved(parts_of(edges[...]), one_hot(index, TABLE))
-
-
-def operator(slabs, metric, turned, across, b):
-    stiff = stiffness()
-    edge_sum = [None] * PTS
+        sides = [
+            jnp.where(
+                lane24 < 2 * BC + BR,
+                turn(west, 2 * BC - (32 * j + 8 * t)),
+                turn(east, 2 * BC + BR - (32 * j + 8 * t)),
+            )
+            for j in range(3)
+        ]
+        sides = jnp.concatenate(sides, axis=0)
+        result.append(jnp.where(lane < 2 * BC, turn(row_in, -32 * t), sides))
+    return result
+
+
+def neighbours(table_ref):
+    return jnp.concatenate([table_ref[s : s + 1, :] for s in range(4)], axis=1)
+
+
+def edge_sums(across, turned, b):
+    sums = [None] * PTS
     for s in range(4):
         raw = [
             across[pl.ds(pl.multiple_of(t * LEV + b * 8, 8), 8), s * ELEM : (s + 1) * ELEM]
@@ -251,7 +275,13 @@
         for t in range(4):
             p = EDGE_POINT[s][t]
             value = jnp.where(turned[s], raw[3 - t], raw[t])
-            edge_sum[p] = value if edge_sum[p] is None else edge_sum[p] + value
+            sums[p] = value if sums[p] is None else sums[p] + value
+    return sums
+
+
+def operator(slabs, metric, turned, across, b):
+    stiff = stiffness()
+    edge_sum = edge_sums(across, turned, b)
     result = []
     for i in range(4):
         for j in range(4):
@@ -275,10 +305,13 @@
 
 def first_kernel(
     tracer_ref, metric_ref, table_ref, below_ref, above_ref, west_ref, east_ref,
-    first_ref, row_ref, col_ref, edges, across,
+    first_ref, row_ref, east_out, west_out, edges, across,
 ):
     fill_edges(edges, lambda p: tracer_ref[pl.ds(p, LEV, stride=PTS), :])
-    gather_across(edges, across, table_ref, (below_ref, above_ref, west_ref, east_ref))
+    halo_in = received((below_ref, above_ref, west_ref, east_ref))
+    for t in range(4):
+        edges[t * LEV : (t + 1) * LEV, 4 * ELEM :] = halo_in[t]
+    across[...] = moved(parts_of(edges[...]), one_hot(neighbours(table_ref), TABLE))
     metric = metric_ref[...]
 
     def block(b, carry):
@@ -291,7 +324,7 @@
 
     lax.fori_loop(0, BLOCKS, block, 0)
     fill_edges(edges, lambda p: first_ref[p])
-    emit(edges, table_ref[8:9, :], row_ref, col_ref)
+    emit(edges, table_ref[8:9, :], row_ref, east_out, west_out)
 
 
 EDGE_SCRATCH = [
@@ -303,9 +336,9 @@
 def first_pass(tracer, metric, table, incoming):
     return pl.pallas_call(
         first_kernel,
-        out_shape=(pltpu.VMEM((PTS, LEV, ELEM), jnp.float32), FLAT, FLAT),
+        out_shape=(pltpu.VMEM((PTS, LEV, ELEM), jnp.float32), FLAT, SIDE, SIDE),
         in_specs=[VMEM] * 7,
-        out_specs=(VMEM, VMEM, VMEM),
+        out_specs=(VMEM,) * 4,
         scratch_shapes=EDGE_SCRATCH,
         compiler_params=PARAMS,
         cost_estimate=cost(2.4),
@@ -313,12 +346,9 @@
     )(*[inside(x) for x in (tracer, metric, table, *incoming)])
 
 
-def second_kernel(
-    tracer_ref, field_ref, metric_ref, table_ref, below_ref, above_ref, west_ref, east_ref,
-    stepped_ref, edges, across,
-):
+def second_kernel(tracer_ref, field_ref, metric_ref, table_ref, stepped_ref, edges, across):
     fill_edges(edges, lambda p: field_ref[p])
-    gather_across(edges, across, table_ref, (below_ref, above_ref, west_ref, east_ref))
+    across[...] = moved(parts_of(edges[...]), one_hot(neighbours(table_ref), 4 * ELEM))
     metric = metric_ref[...]
 
     def block(b, carry):
@@ -333,17 +363,48 @@
     lax.fori_loop(0, BLOCKS, block, 0)
 
 
-def second_pass(tracer, field, metric, table, incoming):
+def second_pass(tracer, field, metric, table):
     return pl.pallas_call(
         second_kernel,
         out_shape=pltpu.VMEM((LEV * PTS, ELEM), jnp.float32),
-        in_specs=[VMEM] * 8,
+        in_specs=[VMEM] * 4,
         out_specs=VMEM,
-        scratch_shapes=EDGE_SCRATCH,
+        scratch_shapes=[pltpu.VMEM((4 * LEV, 4 * ELEM), jnp.float32)] * 2,
         compiler_params=PARAMS,
         cost_estimate=cost(1.2),
         name="second_pass",
-    )(*[inside(x) for x in (tracer, field, metric, table, *incoming)])
+    )(*[inside(x) for x in (tracer, field, metric, table)])
+
+
+def finish_kernel(
+    partial_ref, metric_ref, table_ref, below_ref, above_ref, west_ref, east_ref, stepped_ref, across
+):
+    halo_in = jnp.concatenate(received((below_ref, above_ref, west_ref, east_ref)), axis=0)
+    across[...] = moved(parts_of(halo_in), one_hot(neighbours(table_ref) - 4 * ELEM, ELEM))
+    weight = (HYPER * PENALTY) * metric_ref[...]
+
+    def block(b, carry):
+        sums = edge_sums(across, turned_of(table_ref), b)
+        for p in range(PTS):
+            point = pl.ds(b * (8 * PTS) + p, 8, stride=PTS)
+            value = partial_ref[point, :]
+            stepped_ref[point, :] = value if sums[p] is None else value - weight * sums[p]
+        return carry
+
+    lax.fori_loop(0, BLOCKS, block, 0)
+
+
+def finish(partial, metric, table, incoming):
+    return pl.pallas_call(
+        finish_kernel,
+        out_shape=pltpu.VMEM((LEV * PTS, ELEM), jnp.float32),
+        in_specs=[VMEM] * 7,
+        out_specs=VMEM,
+        scratch_shapes=[pltpu.VMEM((4 * LEV, 4 * ELEM), jnp.float32)],
+        compiler_params=PARAMS,
+        cost_estimate=cost(0.7),
+        name="finish",
+    )(*[inside(x) for x in (partial, metric, table, *incoming)])
 
 
 def mix_kernel(reply_ref, bucket_ref, stepped_ref, out_ref, wide, data, mixing, gain, carried):
@@ -415,28 +476,32 @@
         compiler_params=PARAMS,
         cost_estimate=cost(2.8),
         name="mix",
-    )(inside(replied), inside(bucket), inside(stepped))
-
-
-def exchange(row_out, col_out):
-    def both(value, axis):
+    )(*[inside(x) for x in (replied, bucket, stepped)])
+
+
+def exchange(row_out, east_out, west_out):
+    def moved_by(value, axis, step):
         size = lax.axis_size(axis)
-        up = [(i, (i + 1) % size) for i in range(size)]
-        down = [(j, i) for i, j in up]
-        return lax.ppermute(value, axis, up), lax.ppermute(value, axis, down)
-
-    return both(row_out, "grp") + both(col_out, "dev")
+        return lax.ppermute(value, axis, [(i, (i + step) % size) for i in range(size)])
+
+    return (
+        moved_by(row_out, "grp", 1),
+        moved_by(row_out, "grp", -1),
+        moved_by(east_out, "dev", 1),
+        moved_by(west_out, "dev", -1),
+    )
 
 
 def on_device(tracer, metric, coef, nbr_slot, edge_flip, send_slot, span_slot):
     flat = tracer.reshape(LEV * PTS, ELEM)
     asked, bucket, table, metric = route(span_slot, nbr_slot, edge_flip, send_slot, metric)
-    row_out, col_out = halo(flat, table)
+    outgoing = halo(flat, table)
     got = lax.all_to_all(asked, "dev", split_axis=0, concat_axis=0, tiled=True)
-    incoming = exchange(row_out, col_out)
+    incoming = exchange(*outgoing)
     replied = lax.all_to_all(reply(coef, got), "dev", split_axis=0, concat_axis=0, tiled=True)
-    first, row_out, col_out = first_pass(flat, metric, table, incoming)
-    stepped = second_pass(flat, first, metric, table, exchange(row_out, col_out))
+    first, *outgoing = first_pass(flat, metric, table, incoming)
+    partial = second_pass(flat, first, metric, table)
+    stepped = finish(partial, metric, table, exchange(*outgoing))
     return mix(replied, bucket, stepped)
 
 

time: 65.2 us -> 62.6 us (0.960)
  the two profiles are of different devices: /device:TPU:1 before, /device:TPU:24 now
where the time goes in v3:
time: 62.6 us; the launch traced here: 62.3 us
  starting transfers between devices  46.7 us (75%)
  Pallas kernels  11.6 us (19%)
  waiting for transfers between devices  3.85 us (6%)
    ppermute x8, starting transfers between devices, moved_by(): lax.ppermute(value, axis, [(i, (i + step) % size) for i in range(size)])  23.6 us
    all_to_all x1, starting transfers between devices, on_device(): got = lax.all_to_all(asked, 'dev', split_axis=0, concat_axis=0, tiled=True)  12.7 us
    all_to_all x1, starting transfers between devices, on_device(): lax.all_to_all(reply(coef, got), 'dev', split_axis=0, concat_axis=0, tile...  10.3 us
    ppermute x8, waiting for transfers between devices, moved_by(): lax.ppermute(value, axis, [(i, (i + step) % size) for i in range(size)])  3.84 us
    pallas_call x1, Pallas kernels, mix(): pl.pallas_call(mix_kernel, out_shape=jax.ShapeDtypeStruct((LEV, PTS, ELEM...  2.93 us
    pallas_call x1, Pallas kernels, reply(): pl.pallas_call(reply_kernel, out_shape=pltpu.VMEM((PEERS, BLOCKS, 4, ELEM...  2.35 us
    pallas_call x1, Pallas kernels, route(): pl.pallas_call(route_kernel, out_shape=(pltpu.VMEM((PEERS, 1, ELEM), jnp....  1.98 us
    pallas_call x1, Pallas kernels, first_pass(): pl.pallas_call(first_kernel, out_shape=(pltpu.VMEM((PTS, LEV, ELEM), jnp....  1.97 us
  transfers between devices with their start and end apart: 10, of which 1 were waited for; matrix products, arithmetic and copies ran while one was open for 0% of the time, Pallas kernels for 11%

profile of v3, /device:TPU:24, one launch (start us, length us, event | category | flops | bytes accessed | tf_op | source)
XLA Modules:
  0.0 62.3 jit_solution(13924767687490580383)
XLA Ops:
  0.0 0.0 copy-start.1
  0.0 2.0 %route.1 = (s32[32,1,128]{2,1,0:T(1,128)}, s32[16,128]{1,0:T(8,128)S(1)}, s32[16,128]{1,0:T(8,128)S(1)}, f32[8,128]{1,0:T(8,128)S(1)}) custom-call(s32[16,128]{1,0:T(8,128)} %span_ref.1, s32[4,128]{1,0:T(4,128)} %nbr_ref.1, s32[4,128]{1,0:T(4,128)} %flip_ref.1, s32[1,48]{1,0:T(1,128)} %bitcast.6, f32[1,128]{1,0:T(1,128)} %bitcast.7), custom_call_target="tpu_custom_call" | custom-call | flops 6000000000 | bytes 1048576 | tf_op jit(solution)/shard_map/route/pallas_call | solution.py:210
  2.0 12.7 %all-to-all-start = ((s32[32,1,128]{2,1,0:T(1,128)}), s32[32,1,128]{2,1,0:T(1,128)S(1)}, u32[]{:S(2)}, u32[]{:S(2)}) async-start(s32[32,1,128]{2,1,0:T(1,128)} %get-tuple-element.16), calls=%async_computation | async-start | bytes 32768 | tf_op jit(solution)/shard_map/all_to_all | solution.py:499
  14.7 0.0 copy-done.1
  14.7 0.0 copy-start
  14.7 0.5 halo.1
  15.3 8.8 %collective-permute-start.1 = (f32[72,128]{1,0:T(8,128)S(1)}, f32[72,128]{1,0:T(8,128)S(1)}, u32[]{:S(2)}, u32[]{:S(2)}) collective-permute-start(f32[72,128]{1,0:T(8,128)S(1)} %get-tuple-element.20), channel_id=1, source_target_pairs={{0,736},{32,0},{64,32},{96,64},{128,96},{160,128},{192,160},{224,1... | collective-permute-start | bytes 110600 | tf_op jit(solution)/shard_map/ppermute | solution.py:485
  24.1 0.0 collective-permute-start
  24.1 4.6 %collective-permute-start.2 = (f32[24,128]{1,0:T(8,128)S(1)}, f32[24,128]{1,0:T(8,128)S(1)}, u32[]{:S(2)}, u32[]{:S(2)}) collective-permute-start(f32[24,128]{1,0:T(8,128)S(1)} %get-tuple-element.21), channel_id=1, source_target_pairs={{0,1},{1,2},{2,3},{3,4},{4,5},{5,6},{6,7},{7,8},{8,9},{9,10},{10,1... | collective-permute-start | bytes 36872 | tf_op jit(solution)/shard_map/ppermute | solution.py:485
  28.7 1.9 %collective-permute-start.3 = (f32[24,128]{1,0:T(8,128)S(1)}, f32[24,128]{1,0:T(8,128)S(1)}, u32[]{:S(2)}, u32[]{:S(2)}) collective-permute-start(f32[24,128]{1,0:T(8,128)S(1)} %get-tuple-element.22), channel_id=1, source_target_pairs={{0,31},{1,0},{2,1},{3,2},{4,3},{5,4},{6,5},{7,6},{8,7},{9,8},{10,9... | collective-permute-start | bytes 36872 | tf_op jit(solution)/shard_map/ppermute | solution.py:485
  30.6 0.0 all-to-all-done.got_ref
  30.6 0.0 copy-done
  30.6 2.3 %reply.1 = f32[32,9,4,128]{3,2,1,0:T(4,128)} custom-call(f32[72,2048]{1,0:T(8,128)S(1)} %copy-done, s32[32,1,128]{2,1,0:T(1,128)S(1)} %all-to-all-done.got_ref), custom_call_target="tpu_custom_call" | custom-call | flops 12000000000 | bytes 1048576 | tf_op jit(solution)/shard_map/reply/pallas_call | solution.py:158
  32.9 10.3 %all-to-all-start.1 = ((f32[32,9,4,128]{3,2,1,0:T(4,128)}), f32[32,9,4,128]{3,2,1,0:T(4,128)S(1)}, u32[]{:S(2)}, u32[]{:S(2)}) async-start(f32[32,9,4,128]{3,2,1,0:T(4,128)} %reply.1), calls=%async_computation.1 | async-start | bytes 1179648 | tf_op jit(solution)/shard_map/all_to_all | solution.py:501
  43.3 0.0 collective-permute-done.2.west_ref
  43.3 0.0 collective-permute-done.3.east_ref
  43.3 0.0 collective-permute-done.1.above_ref
  43.3 0.0 collective-permute-done.below_ref
  43.3 2.0 %first_pass.1 = (f32[16,72,128]{2,1,0:T(8,128)S(1)}, f32[72,128]{1,0:T(8,128)S(1)}, f32[24,128]{1,0:T(8,128)S(1)}, f32[24,128]{1,0:T(8,128)S(1)}) custom-call(f32[1152,128]{1,0:T(8,128)S(1)} %bitcast.4, f32[8,128]{1,0:T(8,128)S(1)} %get-tuple-element.18.metric_ref, s32[16,128]{1,0:T(8,128)S(1)} %get-tuple-element.19.table_ref, ...), custom_call_target="tpu_custom_call" | custom-call | flops 12000000000 | bytes 1048576 | tf_op jit(solution)/shard_map/first_pass/pallas_call | solution.py:337
  45.3 1.8 %collective-permute-start.5 = (f32[72,128]{1,0:T(8,128)S(1)}, f32[72,128]{1,0:T(8,128)S(1)}, u32[]{:S(2)}, u32[]{:S(2)}) collective-permute-start(f32[72,128]{1,0:T(8,128)S(1)} %get-tuple-element.24), channel_id=1, source_target_pairs={{0,736},{32,0},{64,32},{96,64},{128,96},{160,128},{192,160},{224,1... | collective-permute-start | bytes 110600 | tf_op jit(solution)/shard_map/ppermute | solution.py:485
  47.1 0.0 collective-permute-start.4
  47.2 4.6 %collective-permute-start.6 = (f32[24,128]{1,0:T(8,128)S(1)}, f32[24,128]{1,0:T(8,128)S(1)}, u32[]{:S(2)}, u32[]{:S(2)}) collective-permute-start(f32[24,128]{1,0:T(8,128)S(1)} %get-tuple-element.25), channel_id=1, source_target_pairs={{0,1},{1,2},{2,3},{3,4},{4,5},{5,6},{6,7},{7,8},{8,9},{9,10},{10,1... | collective-permute-start | bytes 36872 | tf_op jit(solution)/shard_map/ppermute | solution.py:485
  51.7 1.9 %collective-permute-start.7 = (f32[24,128]{1,0:T(8,128)S(1)}, f32[24,128]{1,0:T(8,128)S(1)}, u32[]{:S(2)}, u32[]{:S(2)}) collective-permute-start(f32[24,128]{1,0:T(8,128)S(1)} %get-tuple-element.26), channel_id=1, source_target_pairs={{0,31},{1,0},{2,1},{3,2},{4,3},{5,4},{6,5},{7,6},{8,7},{9,8},{10,9... | collective-permute-start | bytes 36872 | tf_op jit(solution)/shard_map/ppermute | solution.py:485
  53.7 1.0 %second_pass.1.partial_ref = f32[1152,128]{1,0:T(8,128)S(1)} custom-call(f32[1152,128]{1,0:T(8,128)S(1)} %bitcast.5, f32[16,72,128]{2,1,0:T(8,128)S(1)} %get-tuple-element.23.field_ref, f32[8,128]{1,0:T(8,128)S(1)} %get-tuple-element.18.metric_ref, s32[16,128]{1,0:T(8,128)S(1)} %get-tuple-element.19.table_ref), custom_call_target="tpu_custom_call" | custom-call | flops 6000000000 | bytes 1048576 | tf_op jit(solution)/shard_map/second_pass/pallas_call | solution.py:367
  54.7 0.0 collective-permute-done.6.west_ref
  54.7 3.8 %collective-permute-done.7.east_ref = f32[24,128]{1,0:T(8,128)S(1)} collective-permute-done((f32[24,128]{1,0:T(8,128)S(1)}, f32[24,128]{1,0:T(8,128)S(1)}, u32[]{:S(2)}, u32[]{:S(2)}) %collective-permute-start.7) | collective-permute-done | bytes 12320 | tf_op jit(solution)/shard_map/ppermute | solution.py:485
  58.5 0.0 collective-permute-done.5.above_ref
  58.5 0.0 collective-permute-done.4.below_ref
  58.5 0.8 %finish.1.stepped_ref = f32[1152,128]{1,0:T(8,128)S(1)} custom-call(f32[1152,128]{1,0:T(8,128)S(1)} %second_pass.1.partial_ref, f32[8,128]{1,0:T(8,128)S(1)} %get-tuple-element.18.metric_ref, s32[16,128]{1,0:T(8,128)S(1)} %get-tuple-element.19.table_ref, f32[72,128]{1,0:T(8,128)S(1)} %collective-permute-done.4.below_ref, ...), custom_call_target="tpu_custom_call" | custom-call | flops 3500000000 | bytes 1048576 | tf_op jit(solution)/shard_map/finish/pallas_call | solution.py:398
  59.3 0.0 all-to-all-done.1.reply_ref
  59.3 2.9 %mix.1 = f32[72,16,128]{2,1,0:T(8,128)} custom-call(f32[32,9,4,128]{3,2,1,0:T(4,128)S(1)} %all-to-all-done.1.reply_ref, s32[16,128]{1,0:T(8,128)S(1)} %get-tuple-element.17.bucket_ref, f32[1152,128]{1,0:T(8,128)S(1)} %finish.1.stepped_ref), custom_call_target="tpu_custom_call" | custom-call | flops 14000000000 | bytes 1048576 | tf_op jit(solution)/shard_map/mix/pallas_call | solution.py:464
Async XLA Ops:
  0.0 14.7 %copy-start.1 = (f32[72,16,128]{2,1,0:T(8,128)S(1)}, f32[72,16,128]{2,1,0:T(8,128)}, u32[]{:S(2)}) copy-start(f32[72,16,128]{2,1,0:T(8,128)} %param.7) | copy-start | bytes 1769476
  2.0 28.6 %all-to-all-start = ((s32[32,1,128]{2,1,0:T(1,128)}), s32[32,1,128]{2,1,0:T(1,128)S(1)}, u32[]{:S(2)}, u32[]{:S(2)}) async-start(s32[32,1,128]{2,1,0:T(1,128)} %get-tuple-element.16), calls=%async_computation | async-start | bytes 32768 | tf_op jit(solution)/shard_map/all_to_all | solution.py:499
  14.7 15.9 %copy-start = (f32[72,2048]{1,0:T(8,128)S(1)}, f32[72,2048]{1,0:T(8,128)}, u32[]{:S(2)}) copy-start(f32[72,2048]{1,0:T(8,128)} %coef_ref.1) | copy-start | bytes 1769476
  15.3 28.0 %collective-permute-start.1 = (f32[72,128]{1,0:T(8,128)S(1)}, f32[72,128]{1,0:T(8,128)S(1)}, u32[]{:S(2)}, u32[]{:S(2)}) collective-permute-start(f32[72,128]{1,0:T(8,128)S(1)} %get-tuple-element.20), channel_id=1, source_target_pairs={{0,736},{32,0},{64,32},{96,64},{128,96},{160,128},{192,160},{224,1... | collective-permute-start | bytes 110600 | tf_op jit(solution)/shard_map/ppermute | solution.py:485
  24.1 19.3 %collective-permute-start = (f32[72,128]{1,0:T(8,128)S(1)}, f32[72,128]{1,0:T(8,128)S(1)}, u32[]{:S(2)}, u32[]{:S(2)}) collective-permute-start(f32[72,128]{1,0:T(8,128)S(1)} %get-tuple-element.20), channel_id=1, source_target_pairs={{0,32},{32,64},{64,96},{96,128},{128,160},{160,192},{192,224},{224... | collective-permute-start | bytes 110600 | tf_op jit(solution)/shard_map/ppermute | solution.py:485
  24.1 19.2 %collective-permute-start.2 = (f32[24,128]{1,0:T(8,128)S(1)}, f32[24,128]{1,0:T(8,128)S(1)}, u32[]{:S(2)}, u32[]{:S(2)}) collective-permute-start(f32[24,128]{1,0:T(8,128)S(1)} %get-tuple-element.21), channel_id=1, source_target_pairs={{0,1},{1,2},{2,3},{3,4},{4,5},{5,6},{6,7},{7,8},{8,9},{9,10},{10,1... | collective-permute-start | bytes 36872 | tf_op jit(solution)/shard_map/ppermute | solution.py:485
  28.7 14.7 %collective-permute-start.3 = (f32[24,128]{1,0:T(8,128)S(1)}, f32[24,128]{1,0:T(8,128)S(1)}, u32[]{:S(2)}, u32[]{:S(2)}) collective-permute-start(f32[24,128]{1,0:T(8,128)S(1)} %get-tuple-element.22), channel_id=1, source_target_pairs={{0,31},{1,0},{2,1},{3,2},{4,3},{5,4},{6,5},{7,6},{8,7},{9,8},{10,9... | collective-permute-start | bytes 36872 | tf_op jit(solution)/shard_map/ppermute | solution.py:485
  32.9 26.4 %all-to-all-start.1 = ((f32[32,9,4,128]{3,2,1,0:T(4,128)}), f32[32,9,4,128]{3,2,1,0:T(4,128)S(1)}, u32[]{:S(2)}, u32[]{:S(2)}) async-start(f32[32,9,4,128]{3,2,1,0:T(4,128)} %reply.1), calls=%async_computation.1 | async-start | bytes 1179648 | tf_op jit(solution)/shard_map/all_to_all | solution.py:501
  45.3 13.2 %collective-permute-start.5 = (f32[72,128]{1,0:T(8,128)S(1)}, f32[72,128]{1,0:T(8,128)S(1)}, u32[]{:S(2)}, u32[]{:S(2)}) collective-permute-start(f32[72,128]{1,0:T(8,128)S(1)} %get-tuple-element.24), channel_id=1, source_target_pairs={{0,736},{32,0},{64,32},{96,64},{128,96},{160,128},{192,160},{224,1... | collective-permute-start | bytes 110600 | tf_op jit(solution)/shard_map/ppermute | solution.py:485
  47.1 11.4 %collective-permute-start.4 = (f32[72,128]{1,0:T(8,128)S(1)}, f32[72,128]{1,0:T(8,128)S(1)}, u32[]{:S(2)}, u32[]{:S(2)}) collective-permute-start(f32[72,128]{1,0:T(8,128)S(1)} %get-tuple-element.24), channel_id=1, source_target_pairs={{0,32},{32,64},{64,96},{96,128},{128,160},{160,192},{192,224},{224... | collective-permute-start | bytes 110600 | tf_op jit(solution)/shard_map/ppermute | solution.py:485
  47.2 7.5 %collective-permute-start.6 = (f32[24,128]{1,0:T(8,128)S(1)}, f32[24,128]{1,0:T(8,128)S(1)}, u32[]{:S(2)}, u32[]{:S(2)}) collective-permute-start(f32[24,128]{1,0:T(8,128)S(1)} %get-tuple-element.25), channel_id=1, source_target_pairs={{0,1},{1,2},{2,3},{3,4},{4,5},{5,6},{6,7},{7,8},{8,9},{9,10},{10,1... | collective-permute-start | bytes 36872 | tf_op jit(solution)/shard_map/ppermute | solution.py:485
  51.7 6.8 %collective-permute-start.7 = (f32[24,128]{1,0:T(8,128)S(1)}, f32[24,128]{1,0:T(8,128)S(1)}, u32[]{:S(2)}, u32[]{:S(2)}) collective-permute-start(f32[24,128]{1,0:T(8,128)S(1)} %get-tuple-element.26), channel_id=1, source_target_pairs={{0,31},{1,0},{2,1},{3,2},{4,3},{5,4},{6,5},{7,6},{8,7},{9,8},{10,9... | collective-permute-start | bytes 36872 | tf_op jit(solution)/shard_map/ppermute | solution.py:485

commit v4 on v3

--- a/solution.py
+++ b/solution.py
@@ -136,7 +136,8 @@
         req_ref[r] = asked[r : r + 1]
 
 
-def reply_kernel(coef_ref, got_ref, out_ref, data):
+def reply_kernel(coef_ref, got_ref, out_hbm, data, out_ref, done):
+    copies = []
     data[...] = parts_of(coef_ref[...])
     lane = iota((1, ELEM), 1)
     first_half = iota((8, ELEM), 1) < PER
@@ -152,15 +153,27 @@
                 odd = jnp.where(first_half, turned, pltpu.roll(acc[b], 4, 0))
                 out_ref[2 * c, b] = even[:4]
                 out_ref[2 * c + 1, b] = odd[:4]
+        if pair % 2:
+            peers = pl.ds(4 * pair - 4, 8)
+            copies.append(
+                pltpu.make_async_copy(out_ref.at[peers], out_hbm.at[peers], done.at[pair // 2])
+            )
+            copies[-1].start()
+    for copy in copies:
+        copy.wait()
 
 
 def reply(coef, got):
     return pl.pallas_call(
         reply_kernel,
-        out_shape=pltpu.VMEM((PEERS, BLOCKS, 4, ELEM), jnp.float32),
+        out_shape=jax.ShapeDtypeStruct((PEERS, BLOCKS, 4, ELEM), jnp.float32),
         in_specs=[VMEM, VMEM],
-        out_specs=VMEM,
-        scratch_shapes=[pltpu.VMEM((2 * LEV, COLS), jnp.bfloat16)],
+        out_specs=pl.BlockSpec(memory_space=pl.ANY),
+        scratch_shapes=[
+            pltpu.VMEM((2 * LEV, COLS), jnp.bfloat16),
+            pltpu.VMEM((PEERS, BLOCKS, 4, ELEM), jnp.float32),
+            pltpu.SemaphoreType.DMA((4,)),
+        ],
         compiler_params=PARAMS,
         cost_estimate=cost(2.4),
         name="reply",
@@ -322,7 +335,7 @@
             first_ref[p, at, :] = result[p]
         return carry
 
-    lax.fori_loop(0, BLOCKS, block, 0)
+    lax.fori_loop(0, BLOCKS, block, 0, unroll=True)
     fill_edges(edges, lambda p: first_ref[p])
     emit(edges, table_ref[8:9, :], row_ref, east_out, west_out)
 
@@ -360,7 +373,7 @@
             stepped_ref[point, :] = tracer_ref[point, :] - HYPER * result[p]
         return carry
 
-    lax.fori_loop(0, BLOCKS, block, 0)
+    lax.fori_loop(0, BLOCKS, block, 0, unroll=True)
 
 
 def second_pass(tracer, field, metric, table):
@@ -391,7 +404,7 @@
             stepped_ref[point, :] = value if sums[p] is None else value - weight * sums[p]
         return carry
 
-    lax.fori_loop(0, BLOCKS, block, 0)
+    lax.fori_loop(0, BLOCKS, block, 0, unroll=True)
 
 
 def finish(partial, metric, table, incoming):

time: 62.6 us -> 62.1 us (level)
  Pallas kernels: 11.6 us -> 10.9 us
  transfers between devices with their start and end apart: 10 -> 10, of which waited for: 1 -> 1; matrix products, arithmetic and copies ran while one was open for 0% -> 0% of each run, Pallas kernels for 11% -> 10%
where the time goes in v4:
time: 62.1 us; the launch traced here: 61.7 us
  starting transfers between devices  46.7 us (75%)
  Pallas kernels  10.9 us (18%)
  waiting for transfers between devices  3.95 us (6%)
    ppermute x8, starting transfers between devices, moved_by(): lax.ppermute(value, axis, [(i, (i + step) % size) for i in range(size)])  23.6 us
    all_to_all x1, starting transfers between devices, on_device(): got = lax.all_to_all(asked, 'dev', split_axis=0, concat_axis=0, tiled=True)  12.7 us
    all_to_all x1, starting transfers between devices, on_device(): lax.all_to_all(reply(coef, got), 'dev', split_axis=0, concat_axis=0, tile...  10.4 us
    ppermute x8, waiting for transfers between devices, moved_by(): lax.ppermute(value, axis, [(i, (i + step) % size) for i in range(size)])  3.94 us
    pallas_call x1, Pallas kernels, mix(): pl.pallas_call(mix_kernel, out_shape=jax.ShapeDtypeStruct((LEV, PTS, ELEM...  2.93 us
    pallas_call x1, Pallas kernels, reply(): pl.pallas_call(reply_kernel, out_shape=jax.ShapeDtypeStruct((PEERS, BLOCK...  2.23 us
    pallas_call x1, Pallas kernels, route(): pl.pallas_call(route_kernel, out_shape=(pltpu.VMEM((PEERS, 1, ELEM), jnp....  1.98 us
    pallas_call x1, Pallas kernels, first_pass(): pl.pallas_call(first_kernel, out_shape=(pltpu.VMEM((PTS, LEV, ELEM), jnp....  1.61 us
  transfers between devices with their start and end apart: 10, of which 1 were waited for; matrix products, arithmetic and copies ran while one was open for 0% of the time, Pallas kernels for 10%

profile of v4, /device:TPU:24, one launch (start us, length us, event | category | flops | bytes accessed | tf_op | source)
XLA Modules:
  0.0 61.7 jit_solution(13567944770747943380)
XLA Ops:
  0.0 0.0 copy-start.1
  0.0 2.0 %route.1 = (s32[32,1,128]{2,1,0:T(1,128)}, s32[16,128]{1,0:T(8,128)S(1)}, s32[16,128]{1,0:T(8,128)S(1)}, f32[8,128]{1,0:T(8,128)S(1)}) custom-call(s32[16,128]{1,0:T(8,128)} %span_ref.1, s32[4,128]{1,0:T(4,128)} %nbr_ref.1, s32[4,128]{1,0:T(4,128)} %flip_ref.1, s32[1,48]{1,0:T(1,128)} %bitcast.6, f32[1,128]{1,0:T(1,128)} %bitcast.7), custom_call_target="tpu_custom_call" | custom-call | flops 6000000000 | bytes 1048576 | tf_op jit(solution)/shard_map/route/pallas_call | solution.py:223
  2.0 12.7 %all-to-all-start = ((s32[32,1,128]{2,1,0:T(1,128)}), s32[32,1,128]{2,1,0:T(1,128)S(1)}, u32[]{:S(2)}, u32[]{:S(2)}) async-start(s32[32,1,128]{2,1,0:T(1,128)} %get-tuple-element.16), calls=%async_computation | async-start | bytes 32768 | tf_op jit(solution)/shard_map/all_to_all | solution.py:512
  14.7 0.0 copy-done.1
  14.7 0.0 copy-start
  14.7 0.5 halo.1
  15.3 8.8 %collective-permute-start.1 = (f32[72,128]{1,0:T(8,128)S(1)}, f32[72,128]{1,0:T(8,128)S(1)}, u32[]{:S(2)}, u32[]{:S(2)}) collective-permute-start(f32[72,128]{1,0:T(8,128)S(1)} %get-tuple-element.20), channel_id=1, source_target_pairs={{0,736},{32,0},{64,32},{96,64},{128,96},{160,128},{192,160},{224,1... | collective-permute-start | bytes 110600 | tf_op jit(solution)/shard_map/ppermute | solution.py:498
  24.1 0.0 collective-permute-start
  24.1 4.6 %collective-permute-start.2 = (f32[24,128]{1,0:T(8,128)S(1)}, f32[24,128]{1,0:T(8,128)S(1)}, u32[]{:S(2)}, u32[]{:S(2)}) collective-permute-start(f32[24,128]{1,0:T(8,128)S(1)} %get-tuple-element.21), channel_id=1, source_target_pairs={{0,1},{1,2},{2,3},{3,4},{4,5},{5,6},{6,7},{7,8},{8,9},{9,10},{10,1... | collective-permute-start | bytes 36872 | tf_op jit(solution)/shard_map/ppermute | solution.py:498
  28.7 1.9 %collective-permute-start.3 = (f32[24,128]{1,0:T(8,128)S(1)}, f32[24,128]{1,0:T(8,128)S(1)}, u32[]{:S(2)}, u32[]{:S(2)}) collective-permute-start(f32[24,128]{1,0:T(8,128)S(1)} %get-tuple-element.22), channel_id=1, source_target_pairs={{0,31},{1,0},{2,1},{3,2},{4,3},{5,4},{6,5},{7,6},{8,7},{9,8},{10,9... | collective-permute-start | bytes 36872 | tf_op jit(solution)/shard_map/ppermute | solution.py:498
  30.6 0.0 all-to-all-done.got_ref
  30.6 0.0 copy-done
  30.6 2.2 %reply.1 = f32[32,9,4,128]{3,2,1,0:T(4,128)} custom-call(f32[72,2048]{1,0:T(8,128)S(1)} %copy-done, s32[32,1,128]{2,1,0:T(1,128)S(1)} %all-to-all-done.got_ref), custom_call_target="tpu_custom_call" | custom-call | flops 12000000000 | bytes 1048576 | tf_op jit(solution)/shard_map/reply/pallas_call | solution.py:167
  32.8 10.4 %all-to-all-start.1 = ((f32[32,9,4,128]{3,2,1,0:T(4,128)}), f32[32,9,4,128]{3,2,1,0:T(4,128)S(1)}, u32[]{:S(2)}, u32[]{:S(2)}) async-start(f32[32,9,4,128]{3,2,1,0:T(4,128)} %reply.1), calls=%async_computation.1 | async-start | bytes 1179648 | tf_op jit(solution)/shard_map/all_to_all | solution.py:514
  43.2 0.0 collective-permute-done.2.west_ref
  43.2 0.0 collective-permute-done.3.east_ref
  43.2 0.0 collective-permute-done.1.above_ref
  43.2 0.0 collective-permute-done.below_ref
  43.2 1.6 %first_pass.1 = (f32[16,72,128]{2,1,0:T(8,128)S(1)}, f32[72,128]{1,0:T(8,128)S(1)}, f32[24,128]{1,0:T(8,128)S(1)}, f32[24,128]{1,0:T(8,128)S(1)}) custom-call(f32[1152,128]{1,0:T(8,128)S(1)} %bitcast.4, f32[8,128]{1,0:T(8,128)S(1)} %get-tuple-element.18.metric_ref, s32[16,128]{1,0:T(8,128)S(1)} %get-tuple-element.19.table_ref, ...), custom_call_target="tpu_custom_call" | custom-call | flops 12000000000 | bytes 1048576 | tf_op jit(solution)/shard_map/first_pass/pallas_call | solution.py:350
  44.9 1.8 %collective-permute-start.5 = (f32[72,128]{1,0:T(8,128)S(1)}, f32[72,128]{1,0:T(8,128)S(1)}, u32[]{:S(2)}, u32[]{:S(2)}) collective-permute-start(f32[72,128]{1,0:T(8,128)S(1)} %get-tuple-element.24), channel_id=1, source_target_pairs={{0,736},{32,0},{64,32},{96,64},{128,96},{160,128},{192,160},{224,1... | collective-permute-start | bytes 110600 | tf_op jit(solution)/shard_map/ppermute | solution.py:498
  46.7 0.0 collective-permute-start.4
  46.7 4.6 %collective-permute-start.6 = (f32[24,128]{1,0:T(8,128)S(1)}, f32[24,128]{1,0:T(8,128)S(1)}, u32[]{:S(2)}, u32[]{:S(2)}) collective-permute-start(f32[24,128]{1,0:T(8,128)S(1)} %get-tuple-element.25), channel_id=1, source_target_pairs={{0,1},{1,2},{2,3},{3,4},{4,5},{5,6},{6,7},{7,8},{8,9},{9,10},{10,1... | collective-permute-start | bytes 36872 | tf_op jit(solution)/shard_map/ppermute | solution.py:498
  51.3 1.9 %collective-permute-start.7 = (f32[24,128]{1,0:T(8,128)S(1)}, f32[24,128]{1,0:T(8,128)S(1)}, u32[]{:S(2)}, u32[]{:S(2)}) collective-permute-start(f32[24,128]{1,0:T(8,128)S(1)} %get-tuple-element.26), channel_id=1, source_target_pairs={{0,31},{1,0},{2,1},{3,2},{4,3},{5,4},{6,5},{7,6},{8,7},{9,8},{10,9... | collective-permute-start | bytes 36872 | tf_op jit(solution)/shard_map/ppermute | solution.py:498
  53.2 0.9 %second_pass.1.partial_ref = f32[1152,128]{1,0:T(8,128)S(1)} custom-call(f32[1152,128]{1,0:T(8,128)S(1)} %bitcast.5, f32[16,72,128]{2,1,0:T(8,128)S(1)} %get-tuple-element.23.field_ref, f32[8,128]{1,0:T(8,128)S(1)} %get-tuple-element.18.metric_ref, s32[16,128]{1,0:T(8,128)S(1)} %get-tuple-element.19.table_ref), custom_call_target="tpu_custom_call" | custom-call | flops 6000000000 | bytes 1048576 | tf_op jit(solution)/shard_map/second_pass/pallas_call | solution.py:380
  54.1 0.0 collective-permute-done.6.west_ref
  54.2 3.9 %collective-permute-done.7.east_ref = f32[24,128]{1,0:T(8,128)S(1)} collective-permute-done((f32[24,128]{1,0:T(8,128)S(1)}, f32[24,128]{1,0:T(8,128)S(1)}, u32[]{:S(2)}, u32[]{:S(2)}) %collective-permute-start.7) | collective-permute-done | bytes 12320 | tf_op jit(solution)/shard_map/ppermute | solution.py:498
  58.1 0.0 collective-permute-done.5.above_ref
  58.1 0.0 collective-permute-done.4.below_ref
  58.1 0.7 %finish.1.stepped_ref = f32[1152,128]{1,0:T(8,128)S(1)} custom-call(f32[1152,128]{1,0:T(8,128)S(1)} %second_pass.1.partial_ref, f32[8,128]{1,0:T(8,128)S(1)} %get-tuple-element.18.metric_ref, s32[16,128]{1,0:T(8,128)S(1)} %get-tuple-element.19.table_ref, f32[72,128]{1,0:T(8,128)S(1)} %collective-permute-done.4.below_ref, ...), custom_call_target="tpu_custom_call" | custom-call | flops 3500000000 | bytes 1048576 | tf_op jit(solution)/shard_map/finish/pallas_call | solution.py:411
  58.7 0.0 all-to-all-done.1.reply_ref
  58.8 2.9 %mix.1 = f32[72,16,128]{2,1,0:T(8,128)} custom-call(f32[32,9,4,128]{3,2,1,0:T(4,128)S(1)} %all-to-all-done.1.reply_ref, s32[16,128]{1,0:T(8,128)S(1)} %get-tuple-element.17.bucket_ref, f32[1152,128]{1,0:T(8,128)S(1)} %finish.1.stepped_ref), custom_call_target="tpu_custom_call" | custom-call | flops 14000000000 | bytes 1048576 | tf_op jit(solution)/shard_map/mix/pallas_call | solution.py:477
Async XLA Ops:
  0.0 14.7 %copy-start.1 = (f32[72,16,128]{2,1,0:T(8,128)S(1)}, f32[72,16,128]{2,1,0:T(8,128)}, u32[]{:S(2)}) copy-start(f32[72,16,128]{2,1,0:T(8,128)} %param.7) | copy-start | bytes 1769476
  2.0 28.6 %all-to-all-start = ((s32[32,1,128]{2,1,0:T(1,128)}), s32[32,1,128]{2,1,0:T(1,128)S(1)}, u32[]{:S(2)}, u32[]{:S(2)}) async-start(s32[32,1,128]{2,1,0:T(1,128)} %get-tuple-element.16), calls=%async_computation | async-start | bytes 32768 | tf_op jit(solution)/shard_map/all_to_all | solution.py:512
  14.7 15.9 %copy-start = (f32[72,2048]{1,0:T(8,128)S(1)}, f32[72,2048]{1,0:T(8,128)}, u32[]{:S(2)}) copy-start(f32[72,2048]{1,0:T(8,128)} %coef_ref.1) | copy-start | bytes 1769476
  15.3 27.9 %collective-permute-start.1 = (f32[72,128]{1,0:T(8,128)S(1)}, f32[72,128]{1,0:T(8,128)S(1)}, u32[]{:S(2)}, u32[]{:S(2)}) collective-permute-start(f32[72,128]{1,0:T(8,128)S(1)} %get-tuple-element.20), channel_id=1, source_target_pairs={{0,736},{32,0},{64,32},{96,64},{128,96},{160,128},{192,160},{224,1... | collective-permute-start | bytes 110600 | tf_op jit(solution)/shard_map/ppermute | solution.py:498
  24.1 19.2 %collective-permute-start = (f32[72,128]{1,0:T(8,128)S(1)}, f32[72,128]{1,0:T(8,128)S(1)}, u32[]{:S(2)}, u32[]{:S(2)}) collective-permute-start(f32[72,128]{1,0:T(8,128)S(1)} %get-tuple-element.20), channel_id=1, source_target_pairs={{0,32},{32,64},{64,96},{96,128},{128,160},{160,192},{192,224},{224... | collective-permute-start | bytes 110600 | tf_op jit(solution)/shard_map/ppermute | solution.py:498
  24.1 19.1 %collective-permute-start.2 = (f32[24,128]{1,0:T(8,128)S(1)}, f32[24,128]{1,0:T(8,128)S(1)}, u32[]{:S(2)}, u32[]{:S(2)}) collective-permute-start(f32[24,128]{1,0:T(8,128)S(1)} %get-tuple-element.21), channel_id=1, source_target_pairs={{0,1},{1,2},{2,3},{3,4},{4,5},{5,6},{6,7},{7,8},{8,9},{9,10},{10,1... | collective-permute-start | bytes 36872 | tf_op jit(solution)/shard_map/ppermute | solution.py:498
  28.7 14.6 %collective-permute-start.3 = (f32[24,128]{1,0:T(8,128)S(1)}, f32[24,128]{1,0:T(8,128)S(1)}, u32[]{:S(2)}, u32[]{:S(2)}) collective-permute-start(f32[24,128]{1,0:T(8,128)S(1)} %get-tuple-element.22), channel_id=1, source_target_pairs={{0,31},{1,0},{2,1},{3,2},{4,3},{5,4},{6,5},{7,6},{8,7},{9,8},{10,9... | collective-permute-start | bytes 36872 | tf_op jit(solution)/shard_map/ppermute | solution.py:498
  32.8 25.9 %all-to-all-start.1 = ((f32[32,9,4,128]{3,2,1,0:T(4,128)}), f32[32,9,4,128]{3,2,1,0:T(4,128)S(1)}, u32[]{:S(2)}, u32[]{:S(2)}) async-start(f32[32,9,4,128]{3,2,1,0:T(4,128)} %reply.1), calls=%async_computation.1 | async-start | bytes 1179648 | tf_op jit(solution)/shard_map/all_to_all | solution.py:514
  44.9 13.2 %collective-permute-start.5 = (f32[72,128]{1,0:T(8,128)S(1)}, f32[72,128]{1,0:T(8,128)S(1)}, u32[]{:S(2)}, u32[]{:S(2)}) collective-permute-start(f32[72,128]{1,0:T(8,128)S(1)} %get-tuple-element.24), channel_id=1, source_target_pairs={{0,736},{32,0},{64,32},{96,64},{128,96},{160,128},{192,160},{224,1... | collective-permute-start | bytes 110600 | tf_op jit(solution)/shard_map/ppermute | solution.py:498
  46.7 11.4 %collective-permute-start.4 = (f32[72,128]{1,0:T(8,128)S(1)}, f32[72,128]{1,0:T(8,128)S(1)}, u32[]{:S(2)}, u32[]{:S(2)}) collective-permute-start(f32[72,128]{1,0:T(8,128)S(1)} %get-tuple-element.24), channel_id=1, source_target_pairs={{0,32},{32,64},{64,96},{96,128},{128,160},{160,192},{192,224},{224... | collective-permute-start | bytes 110600 | tf_op jit(solution)/shard_map/ppermute | solution.py:498
  46.7 7.4 %collective-permute-start.6 = (f32[24,128]{1,0:T(8,128)S(1)}, f32[24,128]{1,0:T(8,128)S(1)}, u32[]{:S(2)}, u32[]{:S(2)}) collective-permute-start(f32[24,128]{1,0:T(8,128)S(1)} %get-tuple-element.25), channel_id=1, source_target_pairs={{0,1},{1,2},{2,3},{3,4},{4,5},{5,6},{6,7},{7,8},{8,9},{9,10},{10,1... | collective-permute-start | bytes 36872 | tf_op jit(solution)/shard_map/ppermute | solution.py:498
  51.3 6.8 %collective-permute-start.7 = (f32[24,128]{1,0:T(8,128)S(1)}, f32[24,128]{1,0:T(8,128)S(1)}, u32[]{:S(2)}, u32[]{:S(2)}) collective-permute-start(f32[24,128]{1,0:T(8,128)S(1)} %get-tuple-element.26), channel_id=1, source_target_pairs={{0,31},{1,0},{2,1},{3,2},{4,3},{5,4},{6,5},{7,6},{8,7},{9,8},{10,9... | collective-permute-start | bytes 36872 | tf_op jit(solution)/shard_map/ppermute | solution.py:498

commit v5 on v4

--- a/solution.py
+++ b/solution.py
@@ -354,7 +354,7 @@
         out_specs=(VMEM,) * 4,
         scratch_shapes=EDGE_SCRATCH,
         compiler_params=PARAMS,
-        cost_estimate=cost(2.4),
+        cost_estimate=cost(0.3),
         name="first_pass",
     )(*[inside(x) for x in (tracer, metric, table, *incoming)])
 
@@ -384,7 +384,7 @@
         out_specs=VMEM,
         scratch_shapes=[pltpu.VMEM((4 * LEV, 4 * ELEM), jnp.float32)] * 2,
         compiler_params=PARAMS,
-        cost_estimate=cost(1.2),
+        cost_estimate=cost(0.5),
         name="second_pass",
     )(*[inside(x) for x in (tracer, field, metric, table)])
 
@@ -415,7 +415,7 @@
         out_specs=VMEM,
         scratch_shapes=[pltpu.VMEM((4 * LEV, 4 * ELEM), jnp.float32)],
         compiler_params=PARAMS,
-        cost_estimate=cost(0.7),
+        cost_estimate=cost(0.1),
         name="finish",
     )(*[inside(x) for x in (partial, metric, table, *incoming)])
 
@@ -492,16 +492,33 @@
     )(*[inside(x) for x in (replied, bucket, stepped)])
 
 
+def hold_kernel(value_ref, out_ref):
+    out_ref[...] = value_ref[...]
+
+
+def hold(value):
+    return pl.pallas_call(
+        hold_kernel,
+        out_shape=SIDE,
+        in_specs=[VMEM],
+        out_specs=VMEM,
+        compiler_params=PARAMS,
+        cost_estimate=cost(2),
+        name="hold",
+    )(inside(value))
+
+
+def shifted(value, axis, step):
+    size = lax.axis_size(axis)
+    return lax.ppermute(value, axis, [(i, (i + step) % size) for i in range(size)])
+
+
 def exchange(row_out, east_out, west_out):
-    def moved_by(value, axis, step):
-        size = lax.axis_size(axis)
-        return lax.ppermute(value, axis, [(i, (i + step) % size) for i in range(size)])
-
     return (
-        moved_by(row_out, "grp", 1),
-        moved_by(row_out, "grp", -1),
-        moved_by(east_out, "dev", 1),
-        moved_by(west_out, "dev", -1),
+        shifted(row_out, "grp", 1),
+        shifted(row_out, "grp", -1),
+        shifted(east_out, "dev", 1),
+        shifted(west_out, "dev", -1),
     )
 
 
@@ -510,8 +527,10 @@
     asked, bucket, table, metric = route(span_slot, nbr_slot, edge_flip, send_slot, metric)
     outgoing = halo(flat, table)
     got = lax.all_to_all(asked, "dev", split_axis=0, concat_axis=0, tiled=True)
-    incoming = exchange(*outgoing)
-    replied = lax.all_to_all(reply(coef, got), "dev", split_axis=0, concat_axis=0, tiled=True)
+    row_out, east_out, west_out = outgoing
+    sent, west_out = lax.optimization_barrier((reply(coef, got), west_out))
+    incoming = exchange(row_out, east_out, hold(west_out))
+    replied = lax.all_to_all(sent, "dev", split_axis=0, concat_axis=0, tiled=True)
     first, *outgoing = first_pass(flat, metric, table, incoming)
     partial = second_pass(flat, first, metric, table)
     stepped = finish(partial, metric, table, exchange(*outgoing))

time: 62.1 us -> 72.5 us (1.17)
  the two profiles are of different devices: /device:TPU:24 before, /device:TPU:62 now
where the time goes in v5:
time: 72.5 us; the launch traced here: 72.2 us
  starting transfers between devices  49.6 us (68%)
  waiting for transfers between devices  11.5 us (16%)
  Pallas kernels  10.9 us (15%)
    ppermute x8, starting transfers between devices, shifted(): lax.ppermute(value, axis, [(i, (i + step) % size) for i in range(size)])  27.2 us
    all_to_all x1, starting transfers between devices, on_device(): got = lax.all_to_all(asked, 'dev', split_axis=0, concat_axis=0, tiled=True)  12.4 us
    ppermute x8, waiting for transfers between devices, shifted(): lax.ppermute(value, axis, [(i, (i + step) % size) for i in range(size)])  11.5 us
    all_to_all x1, starting transfers between devices, on_device(): lax.all_to_all(sent, 'dev', split_axis=0, concat_axis=0, tiled=True)  9.94 us
    pallas_call x1, Pallas kernels, mix(): pl.pallas_call(mix_kernel, out_shape=jax.ShapeDtypeStruct((LEV, PTS, ELEM...  2.92 us
    pallas_call x1, Pallas kernels, reply(): pl.pallas_call(reply_kernel, out_shape=jax.ShapeDtypeStruct((PEERS, BLOCK...  2.24 us
    pallas_call x1, Pallas kernels, route(): pl.pallas_call(route_kernel, out_shape=(pltpu.VMEM((PEERS, 1, ELEM), jnp....  1.98 us
    pallas_call x1, Pallas kernels, first_pass(): pl.pallas_call(first_kernel, out_shape=(pltpu.VMEM((PTS, LEV, ELEM), jnp....  1.61 us
  transfers between devices with their start and end apart: 10, of which 2 were waited for; matrix products, arithmetic and copies ran while one was open for 0% of the time, Pallas kernels for 8%

profile of v5, /device:TPU:62, one launch (start us, length us, event | category | flops | bytes accessed | tf_op | source)
XLA Modules:
  0.0 72.2 jit_solution(5322047403592125740)
XLA Ops:
  0.0 0.0 copy-start.1
  0.0 2.0 %route.1 = (s32[32,1,128]{2,1,0:T(1,128)}, s32[16,128]{1,0:T(8,128)S(1)}, s32[16,128]{1,0:T(8,128)S(1)}, f32[8,128]{1,0:T(8,128)S(1)}) custom-call(s32[16,128]{1,0:T(8,128)} %span_ref.1, s32[4,128]{1,0:T(4,128)} %nbr_ref.1, s32[4,128]{1,0:T(4,128)} %flip_ref.1, s32[1,48]{1,0:T(1,128)} %bitcast.6, f32[1,128]{1,0:T(1,128)} %bitcast.7), custom_call_target="tpu_custom_call" | custom-call | flops 6000000000 | bytes 1048576 | tf_op jit(solution)/shard_map/route/pallas_call | solution.py:223
  2.0 12.4 %all-to-all-start = ((s32[32,1,128]{2,1,0:T(1,128)}), s32[32,1,128]{2,1,0:T(1,128)S(1)}, u32[]{:S(2)}, u32[]{:S(2)}) async-start(s32[32,1,128]{2,1,0:T(1,128)} %get-tuple-element.18), calls=%async_computation | async-start | bytes 32768 | tf_op jit(solution)/shard_map/all_to_all | solution.py:529
  14.4 0.0 copy-done.1
  14.4 0.0 copy-start
  14.4 0.5 halo.1
  14.9 8.7 %collective-permute-start.1 = (f32[72,128]{1,0:T(8,128)S(1)}, f32[72,128]{1,0:T(8,128)S(1)}, u32[]{:S(2)}, u32[]{:S(2)}) collective-permute-start(f32[72,128]{1,0:T(8,128)S(1)} %get-tuple-element.24), channel_id=1, source_target_pairs={{0,736},{32,0},{64,32},{96,64},{128,96},{160,128},{192,160},{224,1... | collective-permute-start | bytes 110600 | tf_op jit(solution)/shard_map/ppermute | solution.py:513
  23.6 0.0 collective-permute-start
  23.6 2.3 %collective-permute-start.2 = (f32[24,128]{1,0:T(8,128)S(1)}, f32[24,128]{1,0:T(8,128)S(1)}, u32[]{:S(2)}, u32[]{:S(2)}) collective-permute-start(f32[24,128]{1,0:T(8,128)S(1)} %get-tuple-element.25), channel_id=1, source_target_pairs={{0,1},{1,2},{2,3},{3,4},{4,5},{5,6},{6,7},{7,8},{8,9},{9,10},{10,1... | collective-permute-start | bytes 36872 | tf_op jit(solution)/shard_map/ppermute | solution.py:513
  26.0 0.0 all-to-all-done.got_ref
  26.0 0.0 copy-done
  26.0 2.2 %reply.1 = f32[32,9,4,128]{3,2,1,0:T(4,128)} custom-call(f32[72,2048]{1,0:T(8,128)S(1)} %copy-done, s32[32,1,128]{2,1,0:T(1,128)S(1)} %all-to-all-done.got_ref), custom_call_target="tpu_custom_call" | custom-call | flops 12000000000 | bytes 1048576 | tf_op jit(solution)/shard_map/reply/pallas_call | solution.py:167
  28.2 9.9 %all-to-all-start.1 = ((f32[32,9,4,128]{3,2,1,0:T(4,128)}), f32[32,9,4,128]{3,2,1,0:T(4,128)S(1)}, u32[]{:S(2)}, u32[]{:S(2)}) async-start(f32[32,9,4,128]{3,2,1,0:T(4,128)} %reply.1), calls=%async_computation.1 | async-start | bytes 1179648 | tf_op jit(solution)/shard_map/all_to_all | solution.py:533
  38.2 3.4 %collective-permute-start.3 = (f32[24,128]{1,0:T(8,128)S(1)}, f32[24,128]{1,0:T(8,128)S(1)}, u32[]{:S(2)}, u32[]{:S(2)}) collective-permute-start(f32[24,128]{1,0:T(8,128)S(1)} %hold.1), channel_id=1, source_target_pairs={{0,31},{1,0},{2,1},{3,2},{4,3},{5,4},{6,5},{7,6},{8,7},{9,8},{10,9... | collective-permute-start | bytes 36872 | tf_op jit(solution)/shard_map/ppermute | solution.py:513
  41.5 0.0 collective-permute-done.2.west_ref
  41.6 0.0 collective-permute-done.1.above_ref
  41.6 0.0 collective-permute-done.below_ref
  41.6 5.5 %collective-permute-done.3.east_ref = f32[24,128]{1,0:T(8,128)S(1)} collective-permute-done((f32[24,128]{1,0:T(8,128)S(1)}, f32[24,128]{1,0:T(8,128)S(1)}, u32[]{:S(2)}, u32[]{:S(2)}) %collective-permute-start.3) | collective-permute-done | bytes 12320 | tf_op jit(solution)/shard_map/ppermute | solution.py:513
  47.1 1.6 %first_pass.1 = (f32[16,72,128]{2,1,0:T(8,128)S(1)}, f32[72,128]{1,0:T(8,128)S(1)}, f32[24,128]{1,0:T(8,128)S(1)}, f32[24,128]{1,0:T(8,128)S(1)}) custom-call(f32[1152,128]{1,0:T(8,128)S(1)} %bitcast.4, f32[8,128]{1,0:T(8,128)S(1)} %get-tuple-element.23.metric_ref, s32[16,128]{1,0:T(8,128)S(1)} %get-tuple-element.19.table_ref, ...), custom_call_target="tpu_custom_call" | custom-call | flops 1500000000 | bytes 1048576 | tf_op jit(solution)/shard_map/first_pass/pallas_call | solution.py:350
  48.7 6.0 %collective-permute-start.5 = (f32[72,128]{1,0:T(8,128)S(1)}, f32[72,128]{1,0:T(8,128)S(1)}, u32[]{:S(2)}, u32[]{:S(2)}) collective-permute-start(f32[72,128]{1,0:T(8,128)S(1)} %get-tuple-element.28), channel_id=1, source_target_pairs={{0,736},{32,0},{64,32},{96,64},{128,96},{160,128},{192,160},{224,1... | collective-permute-start | bytes 110600 | tf_op jit(solution)/shard_map/ppermute | solution.py:513
  54.7 0.0 collective-permute-start.4
  54.7 5.0 %collective-permute-start.6 = (f32[24,128]{1,0:T(8,128)S(1)}, f32[24,128]{1,0:T(8,128)S(1)}, u32[]{:S(2)}, u32[]{:S(2)}) collective-permute-start(f32[24,128]{1,0:T(8,128)S(1)} %get-tuple-element.29), channel_id=1, source_target_pairs={{0,1},{1,2},{2,3},{3,4},{4,5},{5,6},{6,7},{7,8},{8,9},{9,10},{10,1... | collective-permute-start | bytes 36872 | tf_op jit(solution)/shard_map/ppermute | solution.py:513
  59.7 1.9 %collective-permute-start.7 = (f32[24,128]{1,0:T(8,128)S(1)}, f32[24,128]{1,0:T(8,128)S(1)}, u32[]{:S(2)}, u32[]{:S(2)}) collective-permute-start(f32[24,128]{1,0:T(8,128)S(1)} %get-tuple-element.30), channel_id=1, source_target_pairs={{0,31},{1,0},{2,1},{3,2},{4,3},{5,4},{6,5},{7,6},{8,7},{9,8},{10,9... | collective-permute-start | bytes 36872 | tf_op jit(solution)/shard_map/ppermute | solution.py:513
  61.6 1.0 %second_pass.1.partial_ref = f32[1152,128]{1,0:T(8,128)S(1)} custom-call(f32[1152,128]{1,0:T(8,128)S(1)} %bitcast.5, f32[16,72,128]{2,1,0:T(8,128)S(1)} %get-tuple-element.27.field_ref, f32[8,128]{1,0:T(8,128)S(1)} %get-tuple-element.23.metric_ref, s32[16,128]{1,0:T(8,128)S(1)} %get-tuple-element.19.table_ref), custom_call_target="tpu_custom_call" | custom-call | flops 2500000000 | bytes 1048576 | tf_op jit(solution)/shard_map/second_pass/pallas_call | solution.py:380
  62.6 0.0 collective-permute-done.6.west_ref
  62.6 6.0 %collective-permute-done.7.east_ref = f32[24,128]{1,0:T(8,128)S(1)} collective-permute-done((f32[24,128]{1,0:T(8,128)S(1)}, f32[24,128]{1,0:T(8,128)S(1)}, u32[]{:S(2)}, u32[]{:S(2)}) %collective-permute-start.7) | collective-permute-done | bytes 12320 | tf_op jit(solution)/shard_map/ppermute | solution.py:513
  68.6 0.0 collective-permute-done.5.above_ref
  68.6 0.0 collective-permute-done.4.below_ref
  68.6 0.7 finish.1.stepped_ref
  69.3 0.0 all-to-all-done.1.reply_ref
  69.3 2.9 %mix.1 = f32[72,16,128]{2,1,0:T(8,128)} custom-call(f32[32,9,4,128]{3,2,1,0:T(4,128)S(1)} %all-to-all-done.1.reply_ref, s32[16,128]{1,0:T(8,128)S(1)} %get-tuple-element.22.bucket_ref, f32[1152,128]{1,0:T(8,128)S(1)} %finish.1.stepped_ref), custom_call_target="tpu_custom_call" | custom-call | flops 14000000000 | bytes 1048576 | tf_op jit(solution)/shard_map/mix/pallas_call | solution.py:477
  (1 shorter events, 0.0 us)
Async XLA Ops:
  0.0 14.4 %copy-start.1 = (f32[72,16,128]{2,1,0:T(8,128)S(1)}, f32[72,16,128]{2,1,0:T(8,128)}, u32[]{:S(2)}) copy-start(f32[72,16,128]{2,1,0:T(8,128)} %param.7) | copy-start | bytes 1769476
  2.0 24.0 %all-to-all-start = ((s32[32,1,128]{2,1,0:T(1,128)}), s32[32,1,128]{2,1,0:T(1,128)S(1)}, u32[]{:S(2)}, u32[]{:S(2)}) async-start(s32[32,1,128]{2,1,0:T(1,128)} %get-tuple-element.18), calls=%async_computation | async-start | bytes 32768 | tf_op jit(solution)/shard_map/all_to_all | solution.py:529
  14.4 11.6 %copy-start = (f32[72,2048]{1,0:T(8,128)S(1)}, f32[72,2048]{1,0:T(8,128)}, u32[]{:S(2)}) copy-start(f32[72,2048]{1,0:T(8,128)} %coef_ref.1) | copy-start | bytes 1769476
  14.9 26.6 %collective-permute-start.1 = (f32[72,128]{1,0:T(8,128)S(1)}, f32[72,128]{1,0:T(8,128)S(1)}, u32[]{:S(2)}, u32[]{:S(2)}) collective-permute-start(f32[72,128]{1,0:T(8,128)S(1)} %get-tuple-element.24), channel_id=1, source_target_pairs={{0,736},{32,0},{64,32},{96,64},{128,96},{160,128},{192,160},{224,1... | collective-permute-start | bytes 110600 | tf_op jit(solution)/shard_map/ppermute | solution.py:513
  23.6 17.9 %collective-permute-start = (f32[72,128]{1,0:T(8,128)S(1)}, f32[72,128]{1,0:T(8,128)S(1)}, u32[]{:S(2)}, u32[]{:S(2)}) collective-permute-start(f32[72,128]{1,0:T(8,128)S(1)} %get-tuple-element.24), channel_id=1, source_target_pairs={{0,32},{32,64},{64,96},{96,128},{128,160},{160,192},{192,224},{224... | collective-permute-start | bytes 110600 | tf_op jit(solution)/shard_map/ppermute | solution.py:513
  23.6 17.9 %collective-permute-start.2 = (f32[24,128]{1,0:T(8,128)S(1)}, f32[24,128]{1,0:T(8,128)S(1)}, u32[]{:S(2)}, u32[]{:S(2)}) collective-permute-start(f32[24,128]{1,0:T(8,128)S(1)} %get-tuple-element.25), channel_id=1, source_target_pairs={{0,1},{1,2},{2,3},{3,4},{4,5},{5,6},{6,7},{7,8},{8,9},{9,10},{10,1... | collective-permute-start | bytes 36872 | tf_op jit(solution)/shard_map/ppermute | solution.py:513
  28.2 41.0 %all-to-all-start.1 = ((f32[32,9,4,128]{3,2,1,0:T(4,128)}), f32[32,9,4,128]{3,2,1,0:T(4,128)S(1)}, u32[]{:S(2)}, u32[]{:S(2)}) async-start(f32[32,9,4,128]{3,2,1,0:T(4,128)} %reply.1), calls=%async_computation.1 | async-start | bytes 1179648 | tf_op jit(solution)/shard_map/all_to_all | solution.py:533
  38.2 8.9 %collective-permute-start.3 = (f32[24,128]{1,0:T(8,128)S(1)}, f32[24,128]{1,0:T(8,128)S(1)}, u32[]{:S(2)}, u32[]{:S(2)}) collective-permute-start(f32[24,128]{1,0:T(8,128)S(1)} %hold.1), channel_id=1, source_target_pairs={{0,31},{1,0},{2,1},{3,2},{4,3},{5,4},{6,5},{7,6},{8,7},{9,8},{10,9... | collective-permute-start | bytes 36872 | tf_op jit(solution)/shard_map/ppermute | solution.py:513
  48.7 19.9 %collective-permute-start.5 = (f32[72,128]{1,0:T(8,128)S(1)}, f32[72,128]{1,0:T(8,128)S(1)}, u32[]{:S(2)}, u32[]{:S(2)}) collective-permute-start(f32[72,128]{1,0:T(8,128)S(1)} %get-tuple-element.28), channel_id=1, source_target_pairs={{0,736},{32,0},{64,32},{96,64},{128,96},{160,128},{192,160},{224,1... | collective-permute-start | bytes 110600 | tf_op jit(solution)/shard_map/ppermute | solution.py:513
  54.7 13.9 %collective-permute-start.4 = (f32[72,128]{1,0:T(8,128)S(1)}, f32[72,128]{1,0:T(8,128)S(1)}, u32[]{:S(2)}, u32[]{:S(2)}) collective-permute-start(f32[72,128]{1,0:T(8,128)S(1)} %get-tuple-element.28), channel_id=1, source_target_pairs={{0,32},{32,64},{64,96},{96,128},{128,160},{160,192},{192,224},{224... | collective-permute-start | bytes 110600 | tf_op jit(solution)/shard_map/ppermute | solution.py:513
  54.7 7.9 %collective-permute-start.6 = (f32[24,128]{1,0:T(8,128)S(1)}, f32[24,128]{1,0:T(8,128)S(1)}, u32[]{:S(2)}, u32[]{:S(2)}) collective-permute-start(f32[24,128]{1,0:T(8,128)S(1)} %get-tuple-element.29), channel_id=1, source_target_pairs={{0,1},{1,2},{2,3},{3,4},{4,5},{5,6},{6,7},{7,8},{8,9},{9,10},{10,1... | collective-permute-start | bytes 36872 | tf_op jit(solution)/shard_map/ppermute | solution.py:513
  59.7 8.9 %collective-permute-start.7 = (f32[24,128]{1,0:T(8,128)S(1)}, f32[24,128]{1,0:T(8,128)S(1)}, u32[]{:S(2)}, u32[]{:S(2)}) collective-permute-start(f32[24,128]{1,0:T(8,128)S(1)} %get-tuple-element.30), channel_id=1, source_target_pairs={{0,31},{1,0},{2,1},{3,2},{4,3},{5,4},{6,5},{7,6},{8,7},{9,8},{10,9... | collective-permute-start | bytes 36872 | tf_op jit(solution)/shard_map/ppermute | solution.py:513

commit v6 on v4

--- a/solution.py
+++ b/solution.py
@@ -420,7 +420,7 @@
     )(*[inside(x) for x in (partial, metric, table, *incoming)])
 
 
-def mix_kernel(reply_ref, bucket_ref, stepped_ref, out_ref, wide, data, mixing, gain, carried):
+def mix_kernel(reply_ref, bucket_ref, stepped_ref, out_ref, wide, data, mixing, gain, carried, base, link, right):
     first_half = iota((4, ELEM), 1) < PER
     for c in range(PTS):
         lanes = slice(c * ELEM, (c + 1) * ELEM)
@@ -439,37 +439,75 @@
     def level(ref, k):
         return ref[k * PTS : (k + 1) * PTS, :]
 
-    zero = jnp.zeros((PTS, ELEM), jnp.float32)
-    half = LEV // 2
-    up_gain, up_rhs, down_gain, down_rhs = zero, zero, zero, zero
+    def keep(ref, k, value):
+        ref[k * PTS : (k + 1) * PTS, :] = value
+
+    high = level(mixing, 0)
+    carry = jnp.zeros((PTS, ELEM), jnp.float32)
+    for k in range(1, LEV, 2):
+        here = level(mixing, k)
+        last = k == LEV - 1
+        scale = 1.0 / (1.0 + here if last else 1.0 + here + level(mixing, k + 1))
+        moved_here = level(stepped_ref, k) * scale
+        low = here * scale
+        keep(base, k - 1, 1.0 + high + low)
+        keep(right, k - 1, level(stepped_ref, k - 1) + carry + here * moved_here)
+        keep(base, k, low)
+        keep(right, k, moved_here)
+        if not last:
+            after = level(mixing, k + 1)
+            high = after * scale
+            carry = after * moved_here
+            keep(link, k, high)
+            keep(link, k + 1, high * here)
+
+    half = LEV // 4
+    up_gain = down_gain = up_rhs = down_rhs = None
     for i in range(half):
-        k = i
-        here, after = level(mixing, k), level(mixing, k + 1)
-        scale = 1.0 / (1.0 + after + here * (1.0 - up_gain))
-        up_rhs = (level(stepped_ref, k) + here * up_rhs) * scale
-        up_gain = after * scale
+        k = 2 * i
+        after = level(link, k + 2)
+        total = level(base, k) + after
+        value = level(right, k)
+        if i:
+            here = level(link, k)
+            total = total + here * (1.0 - up_gain)
+            value = value + here * up_rhs
+        scale = 1.0 / total
+        up_rhs, up_gain = value * scale, after * scale
+        m = LEV - 2 - k
+        here = level(link, m)
+        total = level(base, m) + here
+        value = level(right, m)
+        if i:
+            after = level(link, m + 2)
+            total = total + after * (1.0 - down_gain)
+            value = value + after * down_rhs
+        scale = 1.0 / total
+        down_rhs, down_gain = value * scale, here * scale
         if i < half - 1:
-            gain[k * PTS : (k + 1) * PTS, :] = up_gain
-            carried[k * PTS : (k + 1) * PTS, :] = up_rhs
-        m = LEV - 1 - i
-        here = level(mixing, m)
-        after = zero if i == 0 else level(mixing, m + 1)
-        scale = 1.0 / (1.0 + here + after * (1.0 - down_gain))
-        down_rhs = (level(stepped_ref, m) + after * down_rhs) * scale
-        down_gain = here * scale
-        if i < half - 1:
-            gain[m * PTS : (m + 1) * PTS, :] = down_gain
-            carried[m * PTS : (m + 1) * PTS, :] = down_rhs
+            for at, one, two in ((k, up_gain, up_rhs), (m, down_gain, down_rhs)):
+                keep(gain, at, one)
+                keep(carried, at, two)
     upper = (up_rhs + up_gain * down_rhs) / (1.0 - up_gain * down_gain)
     lower = down_rhs + down_gain * upper
-    out_ref[half - 1] = upper
-    out_ref[half] = lower
-    for i in range(half - 2, -1, -1):
-        upper = level(carried, i) + level(gain, i) * upper
-        out_ref[i] = upper
-        m = LEV - 1 - i
-        lower = level(carried, m) + level(gain, m) * lower
-        out_ref[m] = lower
+    middle = LEV // 2 - 2
+    out_ref[middle] = upper
+    out_ref[middle + 2] = lower
+    out_ref[middle + 1] = (
+        level(right, middle + 1) + level(base, middle + 1) * upper + level(link, middle + 1) * lower
+    )
+    for k in range(middle - 2, -1, -2):
+        below = level(carried, k) + level(gain, k) * upper
+        out_ref[k] = below
+        out_ref[k + 1] = level(right, k + 1) + level(base, k + 1) * below + level(link, k + 1) * upper
+        upper = below
+        m = LEV - 2 - k
+        above = level(carried, m) + level(gain, m) * lower
+        out_ref[m] = above
+        out_ref[m - 1] = level(right, m - 1) + level(base, m - 1) * lower + level(link, m - 1) * above
+        lower = above
+    end = LEV - 1
+    out_ref[end] = level(right, end) + level(base, end) * lower
 
 
 def mix(replied, bucket, stepped):
@@ -482,10 +520,8 @@
         scratch_shapes=[
             pltpu.VMEM((LEV, COLS), jnp.float32),
             pltpu.VMEM((2 * LEV, COLS), jnp.bfloat16),
-            pltpu.VMEM((rows, ELEM), jnp.float32),
-            pltpu.VMEM((rows, ELEM), jnp.float32),
-            pltpu.VMEM((rows, ELEM), jnp.float32),
-        ],
+        ]
+        + [pltpu.VMEM((rows, ELEM), jnp.float32)] * 6,
         compiler_params=PARAMS,
         cost_estimate=cost(2.8),
         name="mix",

time: 62.1 us -> 61.9 us (level)
  no operation moved by 1% of the time
where the time goes in v6:
time: 61.9 us; the launch traced here: 61.6 us
  starting transfers between devices  46.7 us (75%)
  Pallas kernels  10.8 us (17%)
  waiting for transfers between devices  3.95 us (6%)
    ppermute x8, starting transfers between devices, moved_by(): lax.ppermute(value, axis, [(i, (i + step) % size) for i in range(size)])  23.6 us
    all_to_all x1, starting transfers between devices, on_device(): got = lax.all_to_all(asked, 'dev', split_axis=0, concat_axis=0, tiled=True)  12.7 us
    all_to_all x1, starting transfers between devices, on_device(): lax.all_to_all(reply(coef, got), 'dev', split_axis=0, concat_axis=0, tile...  10.4 us
    ppermute x8, waiting for transfers between devices, moved_by(): lax.ppermute(value, axis, [(i, (i + step) % size) for i in range(size)])  3.94 us
    pallas_call x1, Pallas kernels, mix(): pl.pallas_call(mix_kernel, out_shape=jax.ShapeDtypeStruct((LEV, PTS, ELEM...  2.82 us
    pallas_call x1, Pallas kernels, reply(): pl.pallas_call(reply_kernel, out_shape=jax.ShapeDtypeStruct((PEERS, BLOCK...  2.23 us
    pallas_call x1, Pallas kernels, route(): pl.pallas_call(route_kernel, out_shape=(pltpu.VMEM((PEERS, 1, ELEM), jnp....  1.98 us
    pallas_call x1, Pallas kernels, first_pass(): pl.pallas_call(first_kernel, out_shape=(pltpu.VMEM((PTS, LEV, ELEM), jnp....  1.61 us
  transfers between devices with their start and end apart: 10, of which 1 were waited for; matrix products, arithmetic and copies ran while one was open for 0% of the time, Pallas kernels for 10%

profile of v6, /device:TPU:24, one launch (start us, length us, event | category | flops | bytes accessed | tf_op | source)
XLA Modules:
  0.0 61.6 jit_solution(14217472126639864309)
XLA Ops:
  0.0 0.0 copy-start.1
  0.0 2.0 %route.1 = (s32[32,1,128]{2,1,0:T(1,128)}, s32[16,128]{1,0:T(8,128)S(1)}, s32[16,128]{1,0:T(8,128)S(1)}, f32[8,128]{1,0:T(8,128)S(1)}) custom-call(s32[16,128]{1,0:T(8,128)} %span_ref.1, s32[4,128]{1,0:T(4,128)} %nbr_ref.1, s32[4,128]{1,0:T(4,128)} %flip_ref.1, s32[1,48]{1,0:T(1,128)} %bitcast.6, f32[1,128]{1,0:T(1,128)} %bitcast.7), custom_call_target="tpu_custom_call" | custom-call | flops 6000000000 | bytes 1048576 | tf_op jit(solution)/shard_map/route/pallas_call | solution.py:223
  2.0 12.7 %all-to-all-start = ((s32[32,1,128]{2,1,0:T(1,128)}), s32[32,1,128]{2,1,0:T(1,128)S(1)}, u32[]{:S(2)}, u32[]{:S(2)}) async-start(s32[32,1,128]{2,1,0:T(1,128)} %get-tuple-element.16), calls=%async_computation | async-start | bytes 32768 | tf_op jit(solution)/shard_map/all_to_all | solution.py:548
  14.7 0.0 copy-done.1
  14.7 0.0 copy-start
  14.7 0.5 halo.1
  15.3 8.8 %collective-permute-start.1 = (f32[72,128]{1,0:T(8,128)S(1)}, f32[72,128]{1,0:T(8,128)S(1)}, u32[]{:S(2)}, u32[]{:S(2)}) collective-permute-start(f32[72,128]{1,0:T(8,128)S(1)} %get-tuple-element.20), channel_id=1, source_target_pairs={{0,736},{32,0},{64,32},{96,64},{128,96},{160,128},{192,160},{224,1... | collective-permute-start | bytes 110600 | tf_op jit(solution)/shard_map/ppermute | solution.py:534
  24.1 0.0 collective-permute-start
  24.1 4.6 %collective-permute-start.2 = (f32[24,128]{1,0:T(8,128)S(1)}, f32[24,128]{1,0:T(8,128)S(1)}, u32[]{:S(2)}, u32[]{:S(2)}) collective-permute-start(f32[24,128]{1,0:T(8,128)S(1)} %get-tuple-element.21), channel_id=1, source_target_pairs={{0,1},{1,2},{2,3},{3,4},{4,5},{5,6},{6,7},{7,8},{8,9},{9,10},{10,1... | collective-permute-start | bytes 36872 | tf_op jit(solution)/shard_map/ppermute | solution.py:534
  28.7 1.9 %collective-permute-start.3 = (f32[24,128]{1,0:T(8,128)S(1)}, f32[24,128]{1,0:T(8,128)S(1)}, u32[]{:S(2)}, u32[]{:S(2)}) collective-permute-start(f32[24,128]{1,0:T(8,128)S(1)} %get-tuple-element.22), channel_id=1, source_target_pairs={{0,31},{1,0},{2,1},{3,2},{4,3},{5,4},{6,5},{7,6},{8,7},{9,8},{10,9... | collective-permute-start | bytes 36872 | tf_op jit(solution)/shard_map/ppermute | solution.py:534
  30.6 0.0 all-to-all-done.got_ref
  30.6 0.0 copy-done
  30.6 2.2 %reply.1 = f32[32,9,4,128]{3,2,1,0:T(4,128)} custom-call(f32[72,2048]{1,0:T(8,128)S(1)} %copy-done, s32[32,1,128]{2,1,0:T(1,128)S(1)} %all-to-all-done.got_ref), custom_call_target="tpu_custom_call" | custom-call | flops 12000000000 | bytes 1048576 | tf_op jit(solution)/shard_map/reply/pallas_call | solution.py:167
  32.8 10.4 %all-to-all-start.1 = ((f32[32,9,4,128]{3,2,1,0:T(4,128)}), f32[32,9,4,128]{3,2,1,0:T(4,128)S(1)}, u32[]{:S(2)}, u32[]{:S(2)}) async-start(f32[32,9,4,128]{3,2,1,0:T(4,128)} %reply.1), calls=%async_computation.1 | async-start | bytes 1179648 | tf_op jit(solution)/shard_map/all_to_all | solution.py:550
  43.2 0.0 collective-permute-done.2.west_ref
  43.2 0.0 collective-permute-done.3.east_ref
  43.2 0.0 collective-permute-done.1.above_ref
  43.2 0.0 collective-permute-done.below_ref
  43.2 1.6 %first_pass.1 = (f32[16,72,128]{2,1,0:T(8,128)S(1)}, f32[72,128]{1,0:T(8,128)S(1)}, f32[24,128]{1,0:T(8,128)S(1)}, f32[24,128]{1,0:T(8,128)S(1)}) custom-call(f32[1152,128]{1,0:T(8,128)S(1)} %bitcast.4, f32[8,128]{1,0:T(8,128)S(1)} %get-tuple-element.18.metric_ref, s32[16,128]{1,0:T(8,128)S(1)} %get-tuple-element.19.table_ref, ...), custom_call_target="tpu_custom_call" | custom-call | flops 12000000000 | bytes 1048576 | tf_op jit(solution)/shard_map/first_pass/pallas_call | solution.py:350
  44.9 1.8 %collective-permute-start.5 = (f32[72,128]{1,0:T(8,128)S(1)}, f32[72,128]{1,0:T(8,128)S(1)}, u32[]{:S(2)}, u32[]{:S(2)}) collective-permute-start(f32[72,128]{1,0:T(8,128)S(1)} %get-tuple-element.24), channel_id=1, source_target_pairs={{0,736},{32,0},{64,32},{96,64},{128,96},{160,128},{192,160},{224,1... | collective-permute-start | bytes 110600 | tf_op jit(solution)/shard_map/ppermute | solution.py:534
  46.7 0.0 collective-permute-start.4
  46.7 4.6 %collective-permute-start.6 = (f32[24,128]{1,0:T(8,128)S(1)}, f32[24,128]{1,0:T(8,128)S(1)}, u32[]{:S(2)}, u32[]{:S(2)}) collective-permute-start(f32[24,128]{1,0:T(8,128)S(1)} %get-tuple-element.25), channel_id=1, source_target_pairs={{0,1},{1,2},{2,3},{3,4},{4,5},{5,6},{6,7},{7,8},{8,9},{9,10},{10,1... | collective-permute-start | bytes 36872 | tf_op jit(solution)/shard_map/ppermute | solution.py:534
  51.3 1.9 %collective-permute-start.7 = (f32[24,128]{1,0:T(8,128)S(1)}, f32[24,128]{1,0:T(8,128)S(1)}, u32[]{:S(2)}, u32[]{:S(2)}) collective-permute-start(f32[24,128]{1,0:T(8,128)S(1)} %get-tuple-element.26), channel_id=1, source_target_pairs={{0,31},{1,0},{2,1},{3,2},{4,3},{5,4},{6,5},{7,6},{8,7},{9,8},{10,9... | collective-permute-start | bytes 36872 | tf_op jit(solution)/shard_map/ppermute | solution.py:534
  53.2 0.9 %second_pass.1.partial_ref = f32[1152,128]{1,0:T(8,128)S(1)} custom-call(f32[1152,128]{1,0:T(8,128)S(1)} %bitcast.5, f32[16,72,128]{2,1,0:T(8,128)S(1)} %get-tuple-element.23.field_ref, f32[8,128]{1,0:T(8,128)S(1)} %get-tuple-element.18.metric_ref, s32[16,128]{1,0:T(8,128)S(1)} %get-tuple-element.19.table_ref), custom_call_target="tpu_custom_call" | custom-call | flops 6000000000 | bytes 1048576 | tf_op jit(solution)/shard_map/second_pass/pallas_call | solution.py:380
  54.1 0.0 collective-permute-done.6.west_ref
  54.2 3.9 %collective-permute-done.7.east_ref = f32[24,128]{1,0:T(8,128)S(1)} collective-permute-done((f32[24,128]{1,0:T(8,128)S(1)}, f32[24,128]{1,0:T(8,128)S(1)}, u32[]{:S(2)}, u32[]{:S(2)}) %collective-permute-start.7) | collective-permute-done | bytes 12320 | tf_op jit(solution)/shard_map/ppermute | solution.py:534
  58.1 0.0 collective-permute-done.5.above_ref
  58.1 0.0 collective-permute-done.4.below_ref
  58.1 0.7 %finish.1.stepped_ref = f32[1152,128]{1,0:T(8,128)S(1)} custom-call(f32[1152,128]{1,0:T(8,128)S(1)} %second_pass.1.partial_ref, f32[8,128]{1,0:T(8,128)S(1)} %get-tuple-element.18.metric_ref, s32[16,128]{1,0:T(8,128)S(1)} %get-tuple-element.19.table_ref, f32[72,128]{1,0:T(8,128)S(1)} %collective-permute-done.4.below_ref, ...), custom_call_target="tpu_custom_call" | custom-call | flops 3500000000 | bytes 1048576 | tf_op jit(solution)/shard_map/finish/pallas_call | solution.py:411
  58.7 0.0 all-to-all-done.1.reply_ref
  58.8 2.8 %mix.1 = f32[72,16,128]{2,1,0:T(8,128)} custom-call(f32[32,9,4,128]{3,2,1,0:T(4,128)S(1)} %all-to-all-done.1.reply_ref, s32[16,128]{1,0:T(8,128)S(1)} %get-tuple-element.17.bucket_ref, f32[1152,128]{1,0:T(8,128)S(1)} %finish.1.stepped_ref), custom_call_target="tpu_custom_call" | custom-call | flops 14000000000 | bytes 1048576 | tf_op jit(solution)/shard_map/mix/pallas_call | solution.py:515
Async XLA Ops:
  0.0 14.7 %copy-start.1 = (f32[72,16,128]{2,1,0:T(8,128)S(1)}, f32[72,16,128]{2,1,0:T(8,128)}, u32[]{:S(2)}) copy-start(f32[72,16,128]{2,1,0:T(8,128)} %param.7) | copy-start | bytes 1769476
  2.0 28.6 %all-to-all-start = ((s32[32,1,128]{2,1,0:T(1,128)}), s32[32,1,128]{2,1,0:T(1,128)S(1)}, u32[]{:S(2)}, u32[]{:S(2)}) async-start(s32[32,1,128]{2,1,0:T(1,128)} %get-tuple-element.16), calls=%async_computation | async-start | bytes 32768 | tf_op jit(solution)/shard_map/all_to_all | solution.py:548
  14.7 15.9 %copy-start = (f32[72,2048]{1,0:T(8,128)S(1)}, f32[72,2048]{1,0:T(8,128)}, u32[]{:S(2)}) copy-start(f32[72,2048]{1,0:T(8,128)} %coef_ref.1) | copy-start | bytes 1769476
  15.3 27.9 %collective-permute-start.1 = (f32[72,128]{1,0:T(8,128)S(1)}, f32[72,128]{1,0:T(8,128)S(1)}, u32[]{:S(2)}, u32[]{:S(2)}) collective-permute-start(f32[72,128]{1,0:T(8,128)S(1)} %get-tuple-element.20), channel_id=1, source_target_pairs={{0,736},{32,0},{64,32},{96,64},{128,96},{160,128},{192,160},{224,1... | collective-permute-start | bytes 110600 | tf_op jit(solution)/shard_map/ppermute | solution.py:534
  24.1 19.2 %collective-permute-start = (f32[72,128]{1,0:T(8,128)S(1)}, f32[72,128]{1,0:T(8,128)S(1)}, u32[]{:S(2)}, u32[]{:S(2)}) collective-permute-start(f32[72,128]{1,0:T(8,128)S(1)} %get-tuple-element.20), channel_id=1, source_target_pairs={{0,32},{32,64},{64,96},{96,128},{128,160},{160,192},{192,224},{224... | collective-permute-start | bytes 110600 | tf_op jit(solution)/shard_map/ppermute | solution.py:534
  24.1 19.1 %collective-permute-start.2 = (f32[24,128]{1,0:T(8,128)S(1)}, f32[24,128]{1,0:T(8,128)S(1)}, u32[]{:S(2)}, u32[]{:S(2)}) collective-permute-start(f32[24,128]{1,0:T(8,128)S(1)} %get-tuple-element.21), channel_id=1, source_target_pairs={{0,1},{1,2},{2,3},{3,4},{4,5},{5,6},{6,7},{7,8},{8,9},{9,10},{10,1... | collective-permute-start | bytes 36872 | tf_op jit(solution)/shard_map/ppermute | solution.py:534
  28.7 14.6 %collective-permute-start.3 = (f32[24,128]{1,0:T(8,128)S(1)}, f32[24,128]{1,0:T(8,128)S(1)}, u32[]{:S(2)}, u32[]{:S(2)}) collective-permute-start(f32[24,128]{1,0:T(8,128)S(1)} %get-tuple-element.22), channel_id=1, source_target_pairs={{0,31},{1,0},{2,1},{3,2},{4,3},{5,4},{6,5},{7,6},{8,7},{9,8},{10,9... | collective-permute-start | bytes 36872 | tf_op jit(solution)/shard_map/ppermute | solution.py:534
  32.8 25.9 %all-to-all-start.1 = ((f32[32,9,4,128]{3,2,1,0:T(4,128)}), f32[32,9,4,128]{3,2,1,0:T(4,128)S(1)}, u32[]{:S(2)}, u32[]{:S(2)}) async-start(f32[32,9,4,128]{3,2,1,0:T(4,128)} %reply.1), calls=%async_computation.1 | async-start | bytes 1179648 | tf_op jit(solution)/shard_map/all_to_all | solution.py:550
  44.9 13.2 %collective-permute-start.5 = (f32[72,128]{1,0:T(8,128)S(1)}, f32[72,128]{1,0:T(8,128)S(1)}, u32[]{:S(2)}, u32[]{:S(2)}) collective-permute-start(f32[72,128]{1,0:T(8,128)S(1)} %get-tuple-element.24), channel_id=1, source_target_pairs={{0,736},{32,0},{64,32},{96,64},{128,96},{160,128},{192,160},{224,1... | collective-permute-start | bytes 110600 | tf_op jit(solution)/shard_map/ppermute | solution.py:534
  46.7 11.4 %collective-permute-start.4 = (f32[72,128]{1,0:T(8,128)S(1)}, f32[72,128]{1,0:T(8,128)S(1)}, u32[]{:S(2)}, u32[]{:S(2)}) collective-permute-start(f32[72,128]{1,0:T(8,128)S(1)} %get-tuple-element.24), channel_id=1, source_target_pairs={{0,32},{32,64},{64,96},{96,128},{128,160},{160,192},{192,224},{224... | collective-permute-start | bytes 110600 | tf_op jit(solution)/shard_map/ppermute | solution.py:534
  46.7 7.4 %collective-permute-start.6 = (f32[24,128]{1,0:T(8,128)S(1)}, f32[24,128]{1,0:T(8,128)S(1)}, u32[]{:S(2)}, u32[]{:S(2)}) collective-permute-start(f32[24,128]{1,0:T(8,128)S(1)} %get-tuple-element.25), channel_id=1, source_target_pairs={{0,1},{1,2},{2,3},{3,4},{4,5},{5,6},{6,7},{7,8},{8,9},{9,10},{10,1... | collective-permute-start | bytes 36872 | tf_op jit(solution)/shard_map/ppermute | solution.py:534
  51.3 6.8 %collective-permute-start.7 = (f32[24,128]{1,0:T(8,128)S(1)}, f32[24,128]{1,0:T(8,128)S(1)}, u32[]{:S(2)}, u32[]{:S(2)}) collective-permute-start(f32[24,128]{1,0:T(8,128)S(1)} %get-tuple-element.26), channel_id=1, source_target_pairs={{0,31},{1,0},{2,1},{3,2},{4,3},{5,4},{6,5},{7,6},{8,7},{9,8},{10,9... | collective-permute-start | bytes 36872 | tf_op jit(solution)/shard_map/ppermute | solution.py:534
